TPU v7x, 32 devices: a whole 2x2x4 slice. The times are simulated.
32 devices in a mesh: groups: 2 (over y), ctx: 16 (over z, x, core).
Axes of the slice: x: 2, y: 2, z: 4, core: 2. Of those that a mesh axis runs over, the one named last changes fastest.
Arguments:
- normed_input: bfloat16 [2048, 8192], P(('groups', 'ctx')), parts along dimension 0, may hold values from -5 to 5
- query_base: bfloat16 [2048, 4096], P(('groups', 'ctx')), parts along dimension 0, may hold values from -6 to 6
- key_base: bfloat16 [2048, 512], P(('groups', 'ctx')), parts along dimension 0, may hold values from -6 to 6
- value_base: bfloat16 [2048, 512], P(('groups', 'ctx')), parts along dimension 0, may hold values from -4 to 4
- adapter_pool: bfloat16 [16, 2686976], P('ctx'), may hold values from -1 to 1
- stretch_adapter: int32 [4], P('groups'), parts along dimension 0, may hold values from 0 to 15
- adapter_owner: int32 [16], replicated, may hold values from 0 to 15, each once
Outputs:
- attended: bfloat16 [2048, 4096], P(('groups', 'ctx')), parts along dimension 0
- out_delta: bfloat16 [2048, 8192], P(('groups', 'ctx')), parts along dimension 0
There are 2 independent parts, one for each index of `groups`. A program takes and returns all parts, laid end to end along the dimension named above; an argument that names none is the same for every part. Nothing has to cross between parts.
All inputs are finite; a program needn't handle non-finite values.
Results may differ from a plain program's by a relative error of at most 0.018.
Values may be sent and summed in bfloat16 or wider, within the bound.
A program may use at most 192 MiB of HBM per device.

v0:
```python
from functools import partial
import math

import jax
import jax.numpy as jnp
from jax import lax
from jax.experimental import pallas as pl
from jax.experimental.pallas import tpu as pltpu
from jax.sharding import PartitionSpec as P

D = 8192
QH = 32
KEYVALUE_HEADS = 4
HEAD_SIZE = 128
ADAPTER_RANK = 64
BLOCK_TOKENS = 512
QKV_POOL = 1900544


adapter_scale = 2.0
rope_base = 500000.0
mask_floor = -1e30


LANES = 128
MESH = pl.DeviceIdType.MESH
ON_CHIP = pl.BlockSpec(memory_space=pltpu.VMEM)
SCALARS = pl.BlockSpec(memory_space=pltpu.SMEM)


def remote(src, dst, send_sem, recv_sem, group, ctx):
    return pltpu.make_async_remote_copy(
        src_ref=src,
        dst_ref=dst,
        send_sem=send_sem,
        recv_sem=recv_sem,
        device_id=(group, ctx),
        device_id_type=MESH,
    )


def place_adapter_kernel(
    groups, cubes, cube,
    pick_ref, x_ref, down_ref, rest_ref,
    x_out, down_out, rest_out,
    down_rows, rest_rows, down_send, rest_send, down_land, rest_land,
    s_cube, r_cube, s_far, r_far, s_tree, r_tree, s_own,
):
    group = lax.axis_index("groups")
    ctx = lax.axis_index("ctx")
    inner = ctx % cube
    outer = ctx // cube
    home = group * cubes + outer
    kinds = groups * cubes
    width = x_out.shape[2] // groups

    barrier = pltpu.get_barrier_semaphore()
    for k in range(1, cube):
        pl.semaphore_signal(
            barrier, inc=1, device_id=(group, outer * cube + (inner ^ k)), device_id_type=MESH
        )
    for k in range(1, kinds):
        there = home ^ k
        pl.semaphore_signal(
            barrier,
            inc=1,
            device_id=(there // cubes, (there % cubes) * cube + inner),
            device_id_type=MESH,
        )
    pl.semaphore_wait(barrier, cube - 1 + kinds - 1)

    sent = []
    down_in, rest_in, x_in = [], [], []

    def columns(part, owner):
        return pl.ds(pl.multiple_of((part * cube + owner) * width, width), width)

    for row, (source, rows, arriving) in enumerate(
        ((down_ref, down_rows, down_in), (rest_ref, rest_rows, rest_in))
    ):
        for k in reversed(range(1, cube)):
            peer = inner ^ k
            copy = remote(
                source.at[peer], rows.at[inner], s_cube.at[row, k], r_cube.at[row, k],
                group, outer * cube + peer,
            )
            copy.start()
            arriving.append(copy)
        own = pltpu.make_async_copy(source.at[inner], rows.at[inner], s_own.at[row])
        own.start()
        own.wait()
    for part in range(groups):
        for k in reversed(range(1, cube)):
            peer = inner ^ k
            copy = remote(
                x_ref.at[:, columns(part, peer)],
                x_out.at[inner, :, pl.ds(part * width, width)],
                s_cube.at[2 + part, k], r_cube.at[2 + part, k],
                group, outer * cube + peer,
            )
            copy.start()
            x_in.append(copy)
        own = pltpu.make_async_copy(
            x_ref.at[:, columns(part, inner)],
            x_out.at[inner, :, pl.ds(part * width, width)],
            s_own.at[2 + part],
        )
        own.start()
        own.wait()

    far = []
    for row, (rows, outgoing, landing, arriving) in enumerate(
        (
            (down_rows, down_send, down_land, down_in),
            (rest_rows, rest_send, rest_land, rest_in),
        )
    ):
        for copy in arriving:
            copy.wait_recv()
        coming = []
        for k in range(1, kinds):
            there = home ^ k
            outgoing[k] = rows[pick_ref[there]]
            copy = remote(
                outgoing.at[k], landing.at[k], s_far.at[row, k], r_far.at[row, k],
                there // cubes, (there % cubes) * cube + inner,
            )
            copy.start()
            coming.append(copy)
        landing[0] = rows[pick_ref[home]]
        far.append(coming)

    for copy in far[0]:
        copy.wait_recv()
    for part in range(groups):
        down_out[part] = down_land[pick_ref[kinds + part]]

    for copy in far[1]:
        copy.wait_recv()
    for part in range(groups):
        rest_out[part, inner] = rest_land[pick_ref[kinds + part]]
    sent = down_in + rest_in + x_in + far[0] + far[1]
    bit = cube // 2
    have = [0]
    tree = {}
    while bit:
        peer = outer * cube + (inner ^ bit)
        new = []
        for k in have:
            for part in range(groups):
                if k & (bit << 1):
                    tree[k, part].wait_recv()
        for k in have:
            for part in range(groups):
                slot = rest_out.at[part, inner ^ k]
                copy = remote(
                    slot, slot, s_tree.at[part, k ^ bit], r_tree.at[part, k ^ bit], group, peer
                )
                copy.start()
                tree[k ^ bit, part] = copy
            new.append(k ^ bit)
        have = have + new
        last = bit
        bit //= 2
    for key, copy in tree.items():
        if key[0] & last:
            copy.wait_recv()
        sent.append(copy)
    for copy in x_in:
        copy.wait_recv()
    for copy in sent:
        copy.wait_send()


def place_adapter(groups, cubes, cube, picks, x, down, rest):
    kinds = groups * cubes
    tokens, depth = x.shape
    down_shape, rest_shape = down.shape[1:], rest.shape[1:]
    bf16 = jnp.bfloat16
    dma = pltpu.SemaphoreType.DMA
    return pl.pallas_call(
        partial(place_adapter_kernel, groups, cubes, cube),
        out_shape=(
            jax.ShapeDtypeStruct((cube, tokens, depth // cube), bf16),
            jax.ShapeDtypeStruct((groups,) + down_shape, bf16),
            jax.ShapeDtypeStruct((groups, cube) + rest_shape, bf16),
        ),
        in_specs=[SCALARS, ON_CHIP, ON_CHIP, ON_CHIP],
        out_specs=(ON_CHIP, ON_CHIP, ON_CHIP),
        scratch_shapes=[
            pltpu.VMEM((cube,) + down_shape, bf16),
            pltpu.VMEM((cube,) + rest_shape, bf16),
            pltpu.VMEM((kinds,) + down_shape, bf16),
            pltpu.VMEM((kinds,) + rest_shape, bf16),
            pltpu.VMEM((kinds,) + down_shape, bf16),
            pltpu.VMEM((kinds,) + rest_shape, bf16),
            dma((2 + groups, cube)),
            dma((2 + groups, cube)),
            dma((2, kinds)),
            dma((2, kinds)),
            dma((groups, cube)),
            dma((groups, cube)),
            dma((2 + groups,)),
        ],
        compiler_params=pltpu.CompilerParams(
            collective_id=0, has_side_effects=True, vmem_limit_bytes=60 * 1024 * 1024
        ),
    )(picks, x, down, rest)


def narrow_kernel(cube, x_ref, w_ref, out_ref, total, outgoing, landing, s_sem, r_sem):
    group = lax.axis_index("groups")
    ctx = lax.axis_index("ctx")
    inner = ctx % cube
    outer = ctx // cube
    barrier = pltpu.get_barrier_semaphore()
    for k in range(1, cube):
        pl.semaphore_signal(
            barrier, inc=1, device_id=(group, outer * cube + (inner ^ k)), device_id_type=MESH
        )
    _, tokens, depth = x_ref.shape
    product = jnp.dot(
        x_ref[...].reshape(cube * tokens, depth), w_ref[...], preferred_element_type=jnp.float32
    ).reshape(cube, tokens, w_ref.shape[1])
    total[...] = product
    outgoing[...] = product.astype(jnp.bfloat16)
    pl.semaphore_wait(barrier, cube - 1)
    copies = []
    for k in range(1, cube):
        peer = inner ^ k
        copy = remote(
            outgoing.at[peer], landing.at[k], s_sem.at[k], r_sem.at[k], group, outer * cube + peer
        )
        copy.start()
        copies.append(copy)
    result = total[inner]
    for k, copy in zip(range(1, cube), copies):
        copy.wait_recv()
        result = result + landing[k].astype(jnp.float32)
    out_ref[...] = result.astype(jnp.bfloat16)
    for copy in copies:
        copy.wait_send()


def narrow(cube, x, w):
    _, tokens, _ = x.shape
    shape = (cube, tokens, w.shape[1])
    return pl.pallas_call(
        partial(narrow_kernel, cube),
        out_shape=jax.ShapeDtypeStruct(shape[1:], jnp.bfloat16),
        in_specs=[ON_CHIP, ON_CHIP],
        out_specs=ON_CHIP,
        scratch_shapes=[
            pltpu.VMEM(shape, jnp.float32),
            pltpu.VMEM(shape, jnp.bfloat16),
            pltpu.VMEM(shape, jnp.bfloat16),
            pltpu.SemaphoreType.DMA((cube,)),
            pltpu.SemaphoreType.DMA((cube,)),
        ],
        compiler_params=pltpu.CompilerParams(collective_id=1, has_side_effects=True),
    )(x, w)


def gather_kernel(count, kv_ref, out_ref, s_sem, r_sem, s_own):
    group = lax.axis_index("groups")
    ctx = lax.axis_index("ctx")
    barrier = pltpu.get_barrier_semaphore()
    levels = count.bit_length() - 1
    for level in range(levels):
        pl.semaphore_signal(
            barrier, inc=1, device_id=(group, ctx ^ (1 << level)), device_id_type=MESH
        )
    own = pltpu.make_async_copy(kv_ref, out_ref.at[ctx], s_own)
    own.start()
    pl.semaphore_wait(barrier, levels)
    own.wait()
    have = [0]
    copies = {}
    for level in reversed(range(levels)):
        bit = 1 << level
        new = []
        for k in have:
            if k and not k & (bit - 1) and k & (bit << 1):
                copies[k].wait_recv()
            slot = out_ref.at[ctx ^ k]
            copy = remote(slot, slot, s_sem.at[k ^ bit], r_sem.at[k ^ bit], group, ctx ^ bit)
            copy.start()
            copies[k ^ bit] = copy
            new.append(k ^ bit)
        have = have + new
    for k, copy in copies.items():
        if k & 1:
            copy.wait_recv()
    for copy in copies.values():
        copy.wait_send()


def gather_rows(count, kv):
    return pl.pallas_call(
        partial(gather_kernel, count),
        out_shape=jax.ShapeDtypeStruct((count,) + kv.shape, kv.dtype),
        in_specs=[ON_CHIP],
        out_specs=ON_CHIP,
        scratch_shapes=[
            pltpu.SemaphoreType.DMA((count,)),
            pltpu.SemaphoreType.DMA((count,)),
            pltpu.SemaphoreType.DMA,
        ],
        compiler_params=pltpu.CompilerParams(
            collective_id=2, has_side_effects=True, vmem_limit_bytes=40 * 1024 * 1024
        ),
    )(kv)


def rotate(delta, token_positions, heads):
    half_dim = HEAD_SIZE // 2
    frequency = rope_base ** (-(jnp.arange(half_dim, dtype=jnp.float32) * 2.0) / HEAD_SIZE)
    angle = token_positions.astype(jnp.float32)[:, None] * frequency[None, :]
    cosine = jnp.cos(angle)[:, None, :]
    sine_part = jnp.sin(angle)[:, None, :]
    shaped = delta.reshape(delta.shape[0], heads, HEAD_SIZE)
    first_half = shaped[..., :half_dim]
    second_half = shaped[..., half_dim:]
    joined = jnp.concatenate(
        [
            first_half * cosine - second_half * sine_part,
            second_half * cosine + first_half * sine_part,
        ],
        -1,
    )
    return joined.reshape(delta.shape[0], heads * HEAD_SIZE)


def project_heads(
    narrow_product, query_row_block, key_row_block, value_row_block, upper_part, token_positions
):
    query_up_weight = upper_part[: ADAPTER_RANK * QH * HEAD_SIZE].reshape(
        ADAPTER_RANK, QH * HEAD_SIZE
    )
    keyvalue_up_weight = upper_part[ADAPTER_RANK * QH * HEAD_SIZE :].reshape(
        ADAPTER_RANK, 2 * KEYVALUE_HEADS * HEAD_SIZE
    )
    query_correction = adapter_scale * jnp.dot(
        narrow_product[:, :ADAPTER_RANK], query_up_weight, preferred_element_type=jnp.float32
    )
    key_correction = adapter_scale * jnp.dot(
        narrow_product[:, ADAPTER_RANK : 2 * ADAPTER_RANK],
        keyvalue_up_weight[:, : KEYVALUE_HEADS * HEAD_SIZE],
        preferred_element_type=jnp.float32,
    )
    value_correction = adapter_scale * jnp.dot(
        narrow_product[:, 2 * ADAPTER_RANK :],
        keyvalue_up_weight[:, KEYVALUE_HEADS * HEAD_SIZE :],
        preferred_element_type=jnp.float32,
    )
    queries = (
        query_row_block.astype(jnp.float32) + rotate(query_correction, token_positions, QH)
    ).astype(jnp.bfloat16)
    new_keys = (
        key_row_block.astype(jnp.float32) + rotate(key_correction, token_positions, KEYVALUE_HEADS)
    ).astype(jnp.bfloat16)
    new_values = (value_row_block.astype(jnp.float32) + value_correction).astype(jnp.bfloat16)
    return (queries, new_keys, new_values)


def output_delta(attended_rows, out_part):
    down_out = out_part[: QH * HEAD_SIZE * ADAPTER_RANK].reshape(QH * HEAD_SIZE, ADAPTER_RANK)
    raised_output = out_part[QH * HEAD_SIZE * ADAPTER_RANK :].reshape(ADAPTER_RANK, D)
    narrow_product = jnp.dot(attended_rows, down_out, preferred_element_type=jnp.float32).astype(
        jnp.bfloat16
    )
    return (
        adapter_scale * jnp.dot(narrow_product, raised_output, preferred_element_type=jnp.float32)
    ).astype(jnp.bfloat16)


def head_major(query_row_block):
    count_rows = query_row_block.shape[0]
    group_size = QH // KEYVALUE_HEADS
    return (
        query_row_block.reshape(count_rows, KEYVALUE_HEADS, group_size, HEAD_SIZE)
        .transpose(1, 2, 0, 3)
        .reshape(KEYVALUE_HEADS, group_size * count_rows, HEAD_SIZE)
    )


def row_major(head_rows, count_rows):
    group_size = QH // KEYVALUE_HEADS
    return (
        head_rows.reshape(KEYVALUE_HEADS, group_size, count_rows, HEAD_SIZE)
        .transpose(2, 0, 1, 3)
        .reshape(count_rows, QH * HEAD_SIZE)
    )


def online_update(current, queries, query_pos, key_slice, value_slice, key_start):
    run_max, run_sum, run_acc = current
    scores = jnp.einsum(
        "hqd,khd->hqk", queries, key_slice, preferred_element_type=jnp.float32
    ) * HEAD_SIZE ** (-0.5)
    key_pos = key_start + jnp.arange(key_slice.shape[0], dtype=jnp.int32)
    allowed = (query_pos[:, None] >= key_pos[None, :])[None]
    new_max = jnp.maximum(run_max, jnp.max(jnp.where(allowed, scores, mask_floor), axis=-1))
    weights = jnp.where(allowed, jnp.exp(scores - new_max[..., None]), 0.0)
    rescale = jnp.exp(run_max - new_max)
    new_sum = run_sum * rescale + jnp.sum(weights, axis=-1)
    new_acc = run_acc * rescale[..., None] + jnp.einsum(
        "hqk,khd->hqd",
        weights.astype(jnp.bfloat16),
        value_slice,
        preferred_element_type=jnp.float32,
    )
    return (new_max, new_sum, new_acc)


def unchanged(current):
    return current


def fold_keys(carry_state, shard_part, prepared):
    key_row_block, value_row_block = shard_part
    key_count = key_row_block.shape[0]
    sub_width = math.gcd(key_count, 1024)
    key_heads = key_row_block.reshape(key_count // sub_width, sub_width, KEYVALUE_HEADS, HEAD_SIZE)
    value_heads = value_row_block.reshape(
        key_count // sub_width, sub_width, KEYVALUE_HEADS, HEAD_SIZE
    )

    def one_step(sub_index, carried):
        key_start = sub_index * sub_width
        key_slice = lax.dynamic_index_in_dim(key_heads, sub_index, 0, keepdims=False)
        value_slice = lax.dynamic_index_in_dim(value_heads, sub_index, 0, keepdims=False)
        updated = []
        for (queries, query_pos), running in zip(prepared, carried):
            advance = partial(
                online_update,
                queries=queries,
                query_pos=query_pos,
                key_slice=key_slice,
                value_slice=value_slice,
                key_start=key_start,
            )
            updated.append(lax.cond(key_start <= jnp.max(query_pos), advance, unchanged, running))
        return tuple(updated)

    return lax.fori_loop(0, key_count // sub_width, one_step, carry_state)


def finish_block(result, count_rows):
    run_max, run_sum, run_acc = result
    divisor = jnp.where(run_sum > 0.0, run_sum, 1.0)
    return row_major(run_acc / divisor[..., None], count_rows).astype(jnp.bfloat16)


def shards(
    normed_input, query_base, key_base, value_base, adapter_pool, stretch_adapter, adapter_owner
):
    cycle_size = lax.axis_size("ctx")
    my_index = lax.axis_index("ctx")
    tok_rows = normed_input.shape[0]
    token_positions = my_index * tok_rows + jnp.arange(tok_rows, dtype=jnp.int32)
    groups = lax.axis_size("groups")
    group = lax.axis_index("groups")
    cube = BLOCK_TOKENS // tok_rows
    cubes = cycle_size // cube
    adapter_ids = jnp.arange(adapter_owner.shape[0], dtype=jnp.int32)
    slots = jnp.sum(
        jnp.where(stretch_adapter[:, None] == adapter_ids[None, :], adapter_owner[None, :], 0),
        axis=1,
    )
    others = [slots]
    for step in range(1, groups):
        route = [(low, low ^ step) for low in range(groups)]
        others.append(lax.ppermute(slots, "groups", route))
    by_step = jnp.stack(others)
    all_slots = jnp.take(
        by_step, jnp.bitwise_xor(group, jnp.arange(groups, dtype=jnp.int32)), axis=0
    )
    my_slot = lax.dynamic_index_in_dim(slots, my_index // cube, 0, keepdims=False)
    home = group * cubes + my_index // cube
    chosen = jnp.bitwise_xor(
        jnp.arange(groups, dtype=jnp.int32) * cubes + my_slot // cube, home
    )
    picks = jnp.concatenate([(all_slots % cube).reshape(-1), chosen]).astype(jnp.int32)
    down_size = 3 * ADAPTER_RANK * D
    rest_size = adapter_pool.shape[1] - down_size
    down_part = lax.dynamic_slice_in_dim(
        adapter_pool[0], group * (down_size // groups), down_size // groups, 0
    ).reshape(cube, -1, LANES)
    rest_part = lax.dynamic_slice_in_dim(
        adapter_pool[0], down_size + group * (rest_size // groups), rest_size // groups, 0
    ).reshape(cube, -1, LANES)
    moved, down_slice, rest = place_adapter(
        groups, cubes, cube, picks, normed_input, down_part, rest_part
    )
    narrow_product = narrow(cube, moved, down_slice.reshape(D // cube, 3 * ADAPTER_RANK))
    rest_row = rest.reshape(-1)
    upper_part = rest_row[: QKV_POOL - down_size]
    out_part = rest_row[QKV_POOL - down_size :]
    queries, new_keys, new_values = project_heads(
        narrow_product, query_base, key_base, value_base, upper_part, token_positions
    )
    group_size = QH // KEYVALUE_HEADS
    blocks = [(queries, token_positions)]
    prepared = [
        (head_major(block_q), jnp.tile(block_pos, group_size)) for block_q, block_pos in blocks
    ]
    initial = tuple(
        (
            (
                jnp.full((KEYVALUE_HEADS, head_q.shape[1]), mask_floor, jnp.float32),
                jnp.zeros((KEYVALUE_HEADS, head_q.shape[1]), jnp.float32),
                jnp.zeros((KEYVALUE_HEADS, head_q.shape[1], HEAD_SIZE), jnp.float32),
            )
            for head_q, block_pos in prepared
        )
    )
    kv_width = KEYVALUE_HEADS * HEAD_SIZE
    gathered = gather_rows(cycle_size, jnp.concatenate([new_keys, new_values], axis=1)).reshape(
        cycle_size * tok_rows, 2 * kv_width
    )
    finals = fold_keys(initial, (gathered[:, :kv_width], gathered[:, kv_width:]), prepared)
    attended = finish_block(finals[0], tok_rows)
    out_delta = output_delta(attended, out_part)
    return (attended, out_delta)


def solution(mesh):
    placed = (
        P(("groups", "ctx"), None),
        P(("groups", "ctx"), None),
        P(("groups", "ctx"), None),
        P(("groups", "ctx"), None),
        P("ctx", None),
        P("groups"),
        P(),
    )
    return jax.shard_map(
        shards,
        mesh=mesh,
        in_specs=placed,
        out_specs=(P(("groups", "ctx"), None), P(("groups", "ctx"), None)),
        check_vma=False,
    )
```

profile of v0, /device:TPU:0, one launch (start us, length us, event | category | flops | bytes accessed | tf_op | source)
XLA Modules:
  0.0 225.5 jit_solution(7349830103586978402)
XLA Ops:
  0.6 0.9 fusion.26
  1.5 3.1 %collective-permute-start = (s32[2]{0:T(128)S(1)}, s32[2]{0:T(128)S(1)}, u32[]{:S(2)}, u32[]{:S(2)}) collective-permute-start(s32[2]{0:T(128)S(1)} %fusion.26), channel_id=1, source_target_pairs={{0,16},{16,0},{1,17},{17,1},{2,18},{18,2},{3,19},{19,3},{4,20},{20... | collective-permute-start | bytes 32 | tf_op jit(solution)/shard_map/ppermute | solution.py:474
  4.5 0.6 dynamic_slice.15
  7.8 28.5 %dynamic-slice_reduce_fusion = bf16[786432]{0:T(1024)(128)(2,1)} fusion(bf16[1,2686976]{1,0:T(2,128)(2,1)} %param.13, s32[]{:T(128)S(6)} %select_n.84), kind=kLoop, calls=%fused_computation.17 | loop fusion | bytes 3145732 | tf_op jit(solution)/shard_map/dynamic_slice | solution.py:487
  36.3 25.1 %dynamic-slice_reduce_fusion.1 = bf16[557056]{0:T(1024)(128)(2,1)} fusion(bf16[1,2686976]{1,0:T(2,128)(2,1)} %param.13, s32[]{:T(128)S(6)} %select_n.85), kind=kLoop, calls=%fused_computation.18 | loop fusion | bytes 2228228 | tf_op jit(solution)/shard_map/dynamic_slice | solution.py:490
  61.4 0.6 broadcast_reduce_fusion
  62.9 1.0 broadcast_in_dim.76
  64.0 0.6 gather_fusion
  64.7 0.6 pad_add_fusion.1.pick_ref
  65.3 84.4 %shard_map.86 = (bf16[8,64,1024]{2,1,0:T(8,128)(2,1)}, bf16[2,768,128]{2,1,0:T(8,128)(2,1)}, bf16[2,8,544,128]{3,2,1,0:T(8,128)(2,1)}) custom-call(s32[6]{0:T(128)} %pad_add_fusion.1.pick_ref, bf16[64,8192]{1,0:T(8,128)(2,1)} %x_ref.1, bf16[8,768,128]{2,1,0:T(8,128)(2,1)} %bitcast.53, bf16[8,544,128]{2,1,0:T(8,128)(2,1)} %bitcast.54), custom_call_target="tpu_custom_call" | custom-call | tf_op jit(solution)/shard_map/pallas_call | solution.py:181
  149.7 4.9 %slice.75 = bf16[1088,1024]{1,0:T(8,128)(2,1)} reshape(bf16[2,8,544,128]{3,2,1,0:T(8,128)(2,1)} %get-tuple-element.111) | data formatting | bytes 4456448 | tf_op jit(solution)/shard_map/slice | solution.py:340
  154.5 2.0 slice.70
  156.5 3.5 %slice.81 = bf16[17408,64]{1,0:T(8,128)(2,1)} reshape(bf16[2,8,544,128]{3,2,1,0:T(8,128)(2,1)S(1)} %copy-done) | data formatting | bytes 4456448 | tf_op jit(solution)/shard_map/slice | solution.py:367
  160.0 2.3 %slice.83 = bf16[136,8192]{1,0:T(8,128)(2,1)} reshape(bf16[2,8,544,128]{3,2,1,0:T(8,128)(2,1)S(1)} %copy-done) | data formatting | bytes 4456448 | tf_op jit(solution)/shard_map/slice | solution.py:368
  162.3 1.2 reshape.198.w_ref
  163.5 10.5 %shard_map.87 = bf16[64,192]{1,0:T(8,128)(2,1)} custom-call(bf16[8,64,1024]{2,1,0:T(8,128)(2,1)} %get-tuple-element.109.x_ref, bf16[1024,192]{1,0:T(8,128)(2,1)} %reshape.198.w_ref), custom_call_target="tpu_custom_call" | custom-call | tf_op jit(solution)/shard_map/pallas_call | solution.py:248
  174.0 1.1 convolution_multiply_fusion.3
  175.2 1.0 fusion.13
  176.5 24.2 %shard_map.88 = bf16[16,64,1024]{2,1,0:T(8,128)(2,1)S(1)} custom-call(bf16[64,1024]{1,0:T(8,128)(2,1)S(1)} %pad_maximum_fusion.2.kv_ref), custom_call_target="tpu_custom_call" | custom-call | tf_op jit(solution)/shard_map/pallas_call | solution.py:299
  200.8 1.3 fusion.11
  202.3 0.4 multiply_subtract_fusion
  203.2 0.7 fusion.18
  204.0 15.9 %conditional.1 = ((f32[4,512]{1,0:T(4,128)S(1)}, f32[4,512,128]{2,1,0:T(8,128)})) conditional(s32[]{:T(128)} %convert_element_type.54, (f32[4,512]{1,0:T(4,128)S(1)}, f32[4,512,128]{2,1,0:T(8,128)}) %tuple.29, (s32[8,64]{1,0:T(8,128)S(1)}, bf16[4,8,64,128]{3,1,0,2:T(8,128)(2,1)S(1)}, bf16[16,64,1024]{2,1,0:T(8,128)(2,1)S(1)}, f32[4,512]{1,0:T(4,128)S(1)}, ...), branch_computations={%region_2.3_spmd, %region_3.6_spmd} | conditional | flops 1097865216 | bytes 79272016 | solution.py:443
  204.5 1.6 fusion.30
  206.0 1.5 copy.21
  207.7 1.8 select_reduce_fusion
  209.6 2.7 %fusion.1 = f32[4,512]{1,0:T(4,128)S(1)} fusion(f32[4,512,1024]{2,1,0:T(8,128)S(1)} %get-tuple-element.134, f32[4,512]{1,0:T(4,128)S(1)} %broadcast_maximum_fusion, pred[512,1024]{1,0:T(8,128)(4,1)S(1)} %iota_compare_fusion), kind=kLoop, calls=%fused_computation.4 | loop fusion | flops 8386560 | bytes 8929280 | tf_op jit(solution)/shard_map/while/body/eval_jaxpr/cond/branch_1_fun/reduce_sum | solution.py:406
  212.3 0.5 copy-done.1
  212.8 0.5 copy.23
  213.4 6.6 %fusion.5 = f32[4,512,128]{2,1,0:T(8,128)} fusion(bf16[1024,4,128]{0,2,1:T(8,128)(2,1)S(1)} %bitcast.63, f32[4,512,1024]{2,1,0:T(8,128)} %copy-done.1, f32[4,512]{1,0:T(4,128)S(1)} %broadcast_maximum_fusion, pred[512,1024]{1,0:T(8,128)(4,1)S(1)} %iota_compare_fusion, f32[4,512,128]{2,1,0:T(8,128)} %get-tuple-element.101, f32[4,512]{1,0:T(4,128)S(1)} %get-tuple-element.131), kind=kOutput, calls=%fused_computation.8 | convolution fusion | flops 545783808 | bytes 12075008 | tf_op jit(solution)/shard_map/while/body/eval_jaxpr/cond/branch_1_fun/hqk,khd->hqd/dot_general | solution.py:407
  219.9 1.6 divide_convert_fusion
  222.1 3.4 %fusion.10 = bf16[64,8192]{1,0:T(8,128)(2,1)} fusion(bf16[64,4096]{1,0:T(8,128)(2,1)S(1)} %bitcast.57, bf16[136,8192]{1,0:T(8,128)(2,1)} %slice.83, bf16[17408,64]{1,0:T(8,128)(2,1)} %slice.81), kind=kOutput, calls=%fused_computation.15 | convolution fusion | flops 101715968 | bytes 3670016 | tf_op jit(solution)/shard_map/dot_general | solution.py:373
  (45 shorter events, 2.8 us)
Async XLA Ops:
  1.5 62.5 %collective-permute-start = (s32[2]{0:T(128)S(1)}, s32[2]{0:T(128)S(1)}, u32[]{:S(2)}, u32[]{:S(2)}) collective-permute-start(s32[2]{0:T(128)S(1)} %fusion.26), channel_id=1, source_target_pairs={{0,16},{16,0},{1,17},{17,1},{2,18},{18,2},{3,19},{19,3},{4,20},{20... | collective-permute-start | bytes 32 | tf_op jit(solution)/shard_map/ppermute | solution.py:474
  149.7 4.9 %copy-start = (bf16[2,8,544,128]{3,2,1,0:T(8,128)(2,1)S(1)}, bf16[2,8,544,128]{3,2,1,0:T(8,128)(2,1)}, u32[]{:S(2)}) copy-start(bf16[2,8,544,128]{3,2,1,0:T(8,128)(2,1)} %get-tuple-element.111) | copy-start | bytes 6684676
  156.5 5.8 %copy-start.5 = (bf16[2,768,128]{2,1,0:T(8,128)(2,1)S(1)}, bf16[2,768,128]{2,1,0:T(8,128)(2,1)}, u32[]{:S(2)}) copy-start(bf16[2,768,128]{2,1,0:T(8,128)(2,1)} %get-tuple-element.110) | copy-start | bytes 1179652
  160.0 15.1 %copy-start.6 = (bf16[64,512]{1,0:T(8,128)(2,1)S(1)}, bf16[64,512]{1,0:T(8,128)(2,1)}, u32[]{:S(2)}) copy-start(bf16[64,512]{1,0:T(8,128)(2,1)} %param.12) | copy-start | bytes 196612
  160.0 16.5 %copy-start.7 = (bf16[64,512]{1,0:T(8,128)(2,1)S(1)}, bf16[64,512]{1,0:T(8,128)(2,1)}, u32[]{:S(2)}) copy-start(bf16[64,512]{1,0:T(8,128)(2,1)} %param.11) | copy-start | bytes 196612
  202.1 1.0 copy-start.4
  209.6 3.2 %copy-start.1 = (f32[4,512,1024]{2,1,0:T(8,128)}, f32[4,512,1024]{2,1,0:T(8,128)S(1)}, u32[]{:S(2)}) copy-start(f32[4,512,1024]{2,1,0:T(8,128)S(1)} %get-tuple-element.134) | copy-start | bytes 25165828 | tf_op jit(solution)/shard_map/while/body/eval_jaxpr/cond
  209.6 3.2 %copy-start.2 = (bf16[1024,512]{1,0:T(8,128)(2,1)S(1)}, bf16[1024,512]{1,0:T(8,128)(2,1)}, u32[]{:S(2)}) copy-start(bf16[1024,512]{1,0:T(8,128)(2,1)} %get-tuple-element.129) | copy-start | bytes 3145732 | tf_op jit(solution)/shard_map/while/body/eval_jaxpr/cond
  222.1 3.4 %copy-start.3 = (bf16[8,8,32,128]{3,1,2,0:T(8,128)(2,1)}, bf16[8,8,32,128]{3,1,2,0:T(8,128)(2,1)S(1)}, u32[]{:S(2)}) copy-start(bf16[8,8,32,128]{3,1,2,0:T(8,128)(2,1)S(1)} %copy.39) | copy-start | bytes 1572868
where the time goes:
time: 226 us
  Pallas kernels  119 us (53%)
  local copies, waits for them, and re-layouts  74.9 us (33%)
  matrix products  15.2 us (7%)
  other arithmetic  8.9 us (4%)
  between operations  4.15 us (2%)
  starting transfers between devices  3.05 us (1%)
    pallas_call x1, Pallas kernels, place_adapter(): pl.pallas_call(partial(place_adapter_kernel, groups, cubes, cube), out_sh...  84.4 us
    dynamic_slice x1, local copies, waits for them, and re-layouts, shards(): lax.dynamic_slice_in_dim(adapter_pool[0], group * (down_size // groups),...  28.5 us
    dynamic_slice x1, local copies, waits for them, and re-layouts, shards(): lax.dynamic_slice_in_dim(adapter_pool[0], down_size + group * (rest_size...  25.1 us
    pallas_call x1, Pallas kernels, gather_rows(): pl.pallas_call(partial(gather_kernel, count), out_shape=jax.ShapeDtypeStr...  24.2 us
    pallas_call x1, Pallas kernels, narrow(): pl.pallas_call(partial(narrow_kernel, cube), out_shape=jax.ShapeDtypeStru...  10.5 us
    dot_general x1, matrix products, online_update(): jnp.einsum('hqk,khd->hqd', weights.astype(jnp.bfloat16), value_slice, pre...  6.55 us
    slice x1, local copies, waits for them, and re-layouts, project_heads(): upper_part[ADAPTER_RANK * QH * HEAD_SIZE:]  4.87 us
  transfers between devices with their start and end apart: 1, of which 0 were waited for; matrix products, arithmetic and copies ran while one was open for 25% of the time, Pallas kernels for 0%

commit v1 on v0

v1 whole, which is shorter than its diff:
```python
from functools import partial
import math

import jax
import jax.numpy as jnp
from jax import lax
from jax.experimental import pallas as pl
from jax.experimental.pallas import tpu as pltpu
from jax.sharding import PartitionSpec as P

D = 8192
QH = 32
KEYVALUE_HEADS = 4
HEAD_SIZE = 128
ADAPTER_RANK = 64
BLOCK_TOKENS = 512
QKV_POOL = 1900544


adapter_scale = 2.0
rope_base = 500000.0
mask_floor = -1e30


LANES = 128
MESH = pl.DeviceIdType.MESH
ON_CHIP = pl.BlockSpec(memory_space=pltpu.VMEM)
SCALARS = pl.BlockSpec(memory_space=pltpu.SMEM)


def remote(src, dst, send_sem, recv_sem, group, ctx):
    return pltpu.make_async_remote_copy(
        src_ref=src,
        dst_ref=dst,
        send_sem=send_sem,
        recv_sem=recv_sem,
        device_id=(group, ctx),
        device_id_type=MESH,
    )


def place_adapter_kernel(
    groups, cubes, cube, down_size,
    pick_ref, x_ref, pool_ref,
    x_out, down_out, rest_out,
    down_flat, rest_flat, down_source, rest_source,
    down_rows, rest_rows, down_send, rest_send, down_land, rest_land,
    s_flat, s_cube, r_cube, s_far, r_far, s_tree, r_tree, s_own,
):
    group = lax.axis_index("groups")
    ctx = lax.axis_index("ctx")
    inner = ctx % cube
    outer = ctx // cube
    home = group * cubes + outer
    kinds = groups * cubes
    width = x_out.shape[2] // groups
    down_piece = down_flat.shape[2]
    rest_piece = rest_flat.shape[2]

    def read_piece(row, k):
        piece = (rest_piece, down_piece)[row]
        start = (group * cube + (inner ^ k)) * piece + (down_size, 0)[row]
        return pltpu.make_async_copy(
            pool_ref.at[:, pl.ds(pl.multiple_of(start, LANES), piece)],
            (rest_flat, down_flat)[row].at[k],
            s_flat.at[row, k],
        )

    for row in range(2):
        for k in reversed(range(cube)):
            read_piece(row, k).start()

    barrier = pltpu.get_barrier_semaphore()
    for k in range(1, cube):
        pl.semaphore_signal(
            barrier, inc=1, device_id=(group, outer * cube + (inner ^ k)), device_id_type=MESH
        )
    for k in range(1, kinds):
        there = home ^ k
        pl.semaphore_signal(
            barrier,
            inc=1,
            device_id=(there // cubes, (there % cubes) * cube + inner),
            device_id_type=MESH,
        )
    pl.semaphore_wait(barrier, cube - 1 + kinds - 1)

    def columns(part, owner):
        return pl.ds(pl.multiple_of((part * cube + owner) * width, width), width)

    def cube_copy(row, k):
        peer = inner ^ k
        return remote(
            (rest_source, down_source)[row].at[k], (rest_rows, down_rows)[row].at[inner],
            s_cube.at[row, k], r_cube.at[row, k], group, outer * cube + peer,
        )

    def dense(row, k):
        flat = (rest_flat, down_flat)[row][k].astype(jnp.float32)
        return flat.reshape(-1, LANES).astype(jnp.bfloat16)

    def x_copy(part, k):
        peer = inner ^ k
        return remote(
            x_ref.at[:, columns(part, peer)],
            x_out.at[inner, :, pl.ds(part * width, width)],
            s_cube.at[2 + part, k], r_cube.at[2 + part, k],
            group, outer * cube + peer,
        )

    for row, (source, rows) in enumerate(((rest_source, rest_rows), (down_source, down_rows))):

        def spread(step, carry, row=row, source=source):
            k = cube - 1 - step
            read_piece(row, k).wait()
            source[k] = dense(row, k)
            cube_copy(row, k).start()
            return carry

        lax.fori_loop(0, cube - 1, spread, 0)
        read_piece(row, 0).wait()
        rows[inner] = dense(row, 0)

    owns = []
    for part in range(groups):
        own = pltpu.make_async_copy(
            x_ref.at[:, columns(part, inner)],
            x_out.at[inner, :, pl.ds(part * width, width)],
            s_own.at[part],
        )
        own.start()
        owns.append(own)

    far = []
    for row, (rows, outgoing, landing) in enumerate(
        ((rest_rows, rest_send, rest_land), (down_rows, down_send, down_land))
    ):
        for k in range(1, cube):
            cube_copy(row, k).wait_recv()
        coming = []
        for k in range(1, kinds):
            there = home ^ k
            outgoing[k] = rows[pick_ref[there]]
            copy = remote(
                outgoing.at[k], landing.at[k], s_far.at[row, k], r_far.at[row, k],
                there // cubes, (there % cubes) * cube + inner,
            )
            copy.start()
            coming.append(copy)
        landing[0] = rows[pick_ref[home]]
        far.append(coming)

    for copy in far[0]:
        copy.wait_recv()
    for part in range(groups):
        rest_out[part, inner] = rest_land[pick_ref[kinds + part]]
    tree = {}
    have = [[0] for _ in range(groups)]
    levels = cube.bit_length() - 1
    orders = []
    for part in range(groups):
        order = [1 << level for level in reversed(range(levels))]
        if part % 2:
            order[:2] = order[1::-1]
        orders.append(order)
    for stage in range(levels):
        for part in range(groups):
            bit = orders[part][stage]
            before = orders[part][stage - 1] if stage else 0
            for k in have[part]:
                if k & before:
                    tree[k, part].wait_recv()
            new = []
            for k in have[part]:
                slot = rest_out.at[part, inner ^ k]
                copy = remote(
                    slot, slot, s_tree.at[part, k ^ bit], r_tree.at[part, k ^ bit],
                    group, outer * cube + (inner ^ bit),
                )
                copy.start()
                tree[k ^ bit, part] = copy
                new.append(k ^ bit)
            have[part] = have[part] + new
        if stage == 0:
            for part in range(groups):
                for k in reversed(range(1, cube)):
                    x_copy(part, k).start()

    for copy in far[1]:
        copy.wait_recv()
    for part in range(groups):
        down_out[part] = down_land[pick_ref[kinds + part]]
    for (k, part), copy in tree.items():
        if k & orders[part][-1]:
            copy.wait_recv()
    for own in owns:
        own.wait()
    for part in range(groups):
        for k in range(1, cube):
            x_copy(part, k).wait_recv()
            x_copy(part, k).wait_send()
    for row in range(2):
        for k in range(1, cube):
            cube_copy(row, k).wait_send()
    for copy in far[0] + far[1] + list(tree.values()):
        copy.wait_send()


def place_adapter(groups, cubes, cube, down_size, picks, x, pool):
    kinds = groups * cubes
    tokens, depth = x.shape
    down_piece = down_size // (groups * cube)
    rest_piece = (pool.shape[1] - down_size) // (groups * cube)
    down_shape = (down_piece // LANES, LANES)
    rest_shape = (rest_piece // LANES, LANES)
    bf16 = jnp.bfloat16
    dma = pltpu.SemaphoreType.DMA
    return pl.pallas_call(
        partial(place_adapter_kernel, groups, cubes, cube, down_size),
        out_shape=(
            jax.ShapeDtypeStruct((cube, tokens, depth // cube), bf16),
            jax.ShapeDtypeStruct((groups,) + down_shape, bf16),
            jax.ShapeDtypeStruct((groups, cube) + rest_shape, bf16),
        ),
        in_specs=[SCALARS, ON_CHIP, pl.BlockSpec(memory_space=pl.ANY)],
        out_specs=(ON_CHIP, ON_CHIP, ON_CHIP),
        scratch_shapes=[
            pltpu.VMEM((cube, 1, down_piece), bf16),
            pltpu.VMEM((cube, 1, rest_piece), bf16),
            pltpu.VMEM((cube,) + down_shape, bf16),
            pltpu.VMEM((cube,) + rest_shape, bf16),
            pltpu.VMEM((cube,) + down_shape, bf16),
            pltpu.VMEM((cube,) + rest_shape, bf16),
            pltpu.VMEM((kinds,) + down_shape, bf16),
            pltpu.VMEM((kinds,) + rest_shape, bf16),
            pltpu.VMEM((kinds,) + down_shape, bf16),
            pltpu.VMEM((kinds,) + rest_shape, bf16),
            dma((2, cube)),
            dma((2 + groups, cube)),
            dma((2 + groups, cube)),
            dma((2, kinds)),
            dma((2, kinds)),
            dma((groups, cube)),
            dma((groups, cube)),
            dma((groups,)),
        ],
        compiler_params=pltpu.CompilerParams(
            collective_id=0, has_side_effects=True, vmem_limit_bytes=60 * 1024 * 1024
        ),
    )(picks, x, pool)


def keyval_kernel(
    cube, count,
    x_ref, w_ref, up_ref, key_ref, value_ref, cos_ref, sin_ref,
    narrow_out, out_ref,
    total, outgoing, landing, s_sem, r_sem, s_all, r_all,
):
    group = lax.axis_index("groups")
    ctx = lax.axis_index("ctx")
    inner = ctx % cube
    outer = ctx // cube
    levels = count.bit_length() - 1
    barrier = pltpu.get_barrier_semaphore()
    apart = list(range(1, cube)) + [1 << n for n in range(levels) if 1 << n >= cube]
    for k in apart:
        pl.semaphore_signal(barrier, inc=1, device_id=(group, ctx ^ k), device_id_type=MESH)
    _, tokens, depth = x_ref.shape
    product = jnp.dot(
        x_ref[...].reshape(cube * tokens, depth), w_ref[...], preferred_element_type=jnp.float32
    ).reshape(cube, tokens, w_ref.shape[1])
    total[...] = product
    outgoing[...] = product.astype(jnp.bfloat16)
    pl.semaphore_wait(barrier, len(apart))
    copies = []
    for k in range(1, cube):
        peer = inner ^ k
        copy = remote(
            outgoing.at[peer], landing.at[k], s_sem.at[k], r_sem.at[k], group, outer * cube + peer
        )
        copy.start()
        copies.append(copy)
    result = total[inner]
    for k, copy in zip(range(1, cube), copies):
        copy.wait_recv()
        result = result + landing[k].astype(jnp.float32)
    low = result.astype(jnp.bfloat16)
    narrow_out[...] = low
    half = HEAD_SIZE // 2
    for j in range(2 * KEYVALUE_HEADS):
        first = ADAPTER_RANK * (1 if j < KEYVALUE_HEADS else 2)
        delta = adapter_scale * jnp.dot(
            low[:, first : first + ADAPTER_RANK], up_ref[j], preferred_element_type=jnp.float32
        )
        base_ref = key_ref if j < KEYVALUE_HEADS else value_ref
        head = j % KEYVALUE_HEADS
        if j < KEYVALUE_HEADS:
            swapped = jnp.concatenate([delta[:, half:], delta[:, :half]], axis=1)
            delta = delta * cos_ref[...] + swapped * sin_ref[...]
        base = base_ref[:, head * HEAD_SIZE : (head + 1) * HEAD_SIZE].astype(jnp.float32)
        out_ref[ctx, :, j * HEAD_SIZE : (j + 1) * HEAD_SIZE] = (base + delta).astype(jnp.bfloat16)
    have = [0]
    moved = {}
    for level in reversed(range(levels)):
        bit = 1 << level
        new = []
        for k in have:
            if k & (bit << 1):
                moved[k].wait_recv()
            slot = out_ref.at[ctx ^ k]
            copy = remote(slot, slot, s_all.at[k ^ bit], r_all.at[k ^ bit], group, ctx ^ bit)
            copy.start()
            moved[k ^ bit] = copy
            new.append(k ^ bit)
        have = have + new
    for k, copy in moved.items():
        if k & 1:
            copy.wait_recv()
    for copy in copies + list(moved.values()):
        copy.wait_send()


def keyval(cube, count, x, w, up, key_rows, value_rows, cosine, sine):
    _, tokens, _ = x.shape
    shape = (cube, tokens, w.shape[1])
    dma = pltpu.SemaphoreType.DMA
    return pl.pallas_call(
        partial(keyval_kernel, cube, count),
        out_shape=(
            jax.ShapeDtypeStruct(shape[1:], jnp.bfloat16),
            jax.ShapeDtypeStruct(
                (count, tokens, 2 * KEYVALUE_HEADS * HEAD_SIZE), jnp.bfloat16
            ),
        ),
        in_specs=[ON_CHIP] * 7,
        out_specs=(ON_CHIP, ON_CHIP),
        scratch_shapes=[
            pltpu.VMEM(shape, jnp.float32),
            pltpu.VMEM(shape, jnp.bfloat16),
            pltpu.VMEM(shape, jnp.bfloat16),
            dma((cube,)),
            dma((cube,)),
            dma((count,)),
            dma((count,)),
        ],
        compiler_params=pltpu.CompilerParams(
            collective_id=1, has_side_effects=True, vmem_limit_bytes=40 * 1024 * 1024
        ),
    )(x, w, up, key_rows, value_rows, cosine, sine)


def attend_kernel(
    step_keys, narrow_ref, query_ref, kv_ref, rest_ref, cos_ref, sin_ref,
    attended_ref, delta_ref,
    wide, queries, permuted, run_max, run_sum, run_acc,
):
    tokens = narrow_ref.shape[0]
    ctx = lax.axis_index("ctx")
    heads = QH // KEYVALUE_HEADS
    rows = heads * tokens
    half = HEAD_SIZE // 2
    query_rows = ADAPTER_RANK * QH
    out_start = query_rows + 2 * ADAPTER_RANK * KEYVALUE_HEADS
    raise_start = out_start + QH * half
    wide[...] = rest_ref[...].astype(jnp.float32)
    low = narrow_ref[:, :ADAPTER_RANK]
    for head in range(QH):
        up = wide[pl.ds(head, ADAPTER_RANK, stride=QH), :].astype(jnp.bfloat16)
        delta = adapter_scale * jnp.dot(low, up, preferred_element_type=jnp.float32)
        delta = delta * cos_ref[...] + pltpu.roll(delta, half, 1) * sin_ref[...]
        base = query_ref[:, head * HEAD_SIZE : (head + 1) * HEAD_SIZE].astype(jnp.float32)
        queries[head // heads, pl.ds((head % heads) * tokens, tokens), :] = (base + delta).astype(
            jnp.bfloat16
        )
    first = ctx * tokens
    steps = (first + tokens + step_keys - 1) // step_keys
    row = lax.broadcasted_iota(jnp.int32, (rows, step_keys), 0)
    query_pos = first + lax.rem(row, tokens)
    key_off = lax.broadcasted_iota(jnp.int32, (rows, step_keys), 1)
    source = lax.broadcasted_iota(jnp.int32, (HEAD_SIZE, HEAD_SIZE), 0)
    target = lax.broadcasted_iota(jnp.int32, (HEAD_SIZE, HEAD_SIZE), 1)
    wanted = jnp.where(target < half, 2 * target, 2 * (target - half) + 1)
    shuffle = jnp.where(source == wanted, 1.0, 0.0).astype(jnp.bfloat16)
    for group in range(KEYVALUE_HEADS):
        run_max[...] = jnp.full_like(run_max, mask_floor)
        run_sum[...] = jnp.zeros_like(run_sum)
        run_acc[...] = jnp.zeros_like(run_acc)
        key_cols = slice(group * HEAD_SIZE, (group + 1) * HEAD_SIZE)
        value_first = (KEYVALUE_HEADS + group) * HEAD_SIZE

        def advance(step, carry):
            start = pl.multiple_of(step * step_keys, step_keys)
            keys = kv_ref[pl.ds(start, step_keys), key_cols]
            values = kv_ref[pl.ds(start, step_keys), value_first : value_first + HEAD_SIZE]
            scores = lax.dot_general(
                queries[group], keys, (((1,), (1,)), ((), ())),
                preferred_element_type=jnp.float32,
            ) * HEAD_SIZE ** (-0.5)
            scores = jnp.where(query_pos >= key_off + start, scores, mask_floor)
            new_max = jnp.maximum(run_max[...], jnp.max(scores, axis=1, keepdims=True))
            weights = jnp.exp(scores - new_max)
            rescale = jnp.exp(run_max[...] - new_max)
            run_sum[...] = run_sum[...] * rescale + jnp.sum(weights, axis=1, keepdims=True)
            run_acc[...] = run_acc[...] * rescale + jnp.dot(
                weights.astype(jnp.bfloat16), values, preferred_element_type=jnp.float32
            )
            run_max[...] = new_max
            return carry

        lax.fori_loop(0, steps, advance, 0)
        result = (run_acc[...] / run_sum[...]).astype(jnp.bfloat16)
        mixed = jnp.dot(result, shuffle, preferred_element_type=jnp.float32).astype(jnp.bfloat16)
        for j in range(heads):
            head = group * heads + j
            cols = slice(head * HEAD_SIZE, (head + 1) * HEAD_SIZE)
            attended_ref[:, cols] = result[j * tokens : (j + 1) * tokens]
            permuted[:, cols] = mixed[j * tokens : (j + 1) * tokens]
    narrow = jnp.zeros((tokens, ADAPTER_RANK), jnp.float32)
    for head in range(QH):
        block = rest_ref[out_start + head * half : out_start + (head + 1) * half, :]
        weight = jnp.concatenate([block[:, :half], block[:, half:]], axis=0)
        narrow = narrow + jnp.dot(
            permuted[:, head * HEAD_SIZE : (head + 1) * HEAD_SIZE],
            weight,
            preferred_element_type=jnp.float32,
        )
    narrow = narrow.astype(jnp.bfloat16)
    blocks = D // LANES
    for j in range(blocks):
        up = wide[pl.ds(raise_start + j, ADAPTER_RANK, stride=blocks), :].astype(jnp.bfloat16)
        delta_ref[:, j * LANES : (j + 1) * LANES] = (
            adapter_scale * jnp.dot(narrow, up, preferred_element_type=jnp.float32)
        ).astype(jnp.bfloat16)


def attend(narrow, query_rows, kv, rest, cosine, sine):
    tokens = narrow.shape[0]
    rows = QH // KEYVALUE_HEADS * tokens
    return pl.pallas_call(
        partial(attend_kernel, math.gcd(kv.shape[0], 1024)),
        out_shape=(
            jax.ShapeDtypeStruct((tokens, QH * HEAD_SIZE), jnp.bfloat16),
            jax.ShapeDtypeStruct((tokens, D), jnp.bfloat16),
        ),
        in_specs=[ON_CHIP] * 6,
        out_specs=(ON_CHIP, ON_CHIP),
        scratch_shapes=[
            pltpu.VMEM(rest.shape, jnp.float32),
            pltpu.VMEM((KEYVALUE_HEADS, rows, HEAD_SIZE), jnp.bfloat16),
            pltpu.VMEM((tokens, QH * HEAD_SIZE), jnp.bfloat16),
            pltpu.VMEM((rows, 1), jnp.float32),
            pltpu.VMEM((rows, 1), jnp.float32),
            pltpu.VMEM((rows, HEAD_SIZE), jnp.float32),
        ],
        compiler_params=pltpu.CompilerParams(vmem_limit_bytes=56 * 1024 * 1024),
    )(narrow, query_rows, kv, rest, cosine, sine)


def shards(
    normed_input, query_base, key_base, value_base, adapter_pool, stretch_adapter, adapter_owner
):
    cycle_size = lax.axis_size("ctx")
    my_index = lax.axis_index("ctx")
    tok_rows = normed_input.shape[0]
    token_positions = my_index * tok_rows + jnp.arange(tok_rows, dtype=jnp.int32)
    groups = lax.axis_size("groups")
    group = lax.axis_index("groups")
    cube = BLOCK_TOKENS // tok_rows
    cubes = cycle_size // cube
    adapter_ids = jnp.arange(adapter_owner.shape[0], dtype=jnp.int32)
    slots = jnp.sum(
        jnp.where(stretch_adapter[:, None] == adapter_ids[None, :], adapter_owner[None, :], 0),
        axis=1,
    )
    others = [slots]
    for step in range(1, groups):
        route = [(low, low ^ step) for low in range(groups)]
        others.append(lax.ppermute(slots, "groups", route))
    by_step = jnp.stack(others)
    all_slots = jnp.take(
        by_step, jnp.bitwise_xor(group, jnp.arange(groups, dtype=jnp.int32)), axis=0
    )
    my_slot = lax.dynamic_index_in_dim(slots, my_index // cube, 0, keepdims=False)
    home = group * cubes + my_index // cube
    chosen = jnp.bitwise_xor(
        jnp.arange(groups, dtype=jnp.int32) * cubes + my_slot // cube, home
    )
    picks = jnp.concatenate([(all_slots % cube).reshape(-1), chosen]).astype(jnp.int32)
    down_size = 3 * ADAPTER_RANK * D
    half_dim = HEAD_SIZE // 2
    frequency = rope_base ** (-(jnp.arange(half_dim, dtype=jnp.float32) * 2.0) / HEAD_SIZE)
    angle = token_positions.astype(jnp.float32)[:, None] * frequency[None, :]
    cosine = jnp.cos(angle)
    sine = jnp.sin(angle)
    cosine = jnp.concatenate([cosine, cosine], axis=1)
    sine = jnp.concatenate([-sine, sine], axis=1)
    moved, down_slice, rest = place_adapter(
        groups, cubes, cube, down_size, picks, normed_input, adapter_pool
    )
    rest = rest.reshape(-1, LANES)
    query_part = ADAPTER_RANK * QH
    keyval_up = (
        rest[query_part : query_part + 2 * ADAPTER_RANK * KEYVALUE_HEADS]
        .reshape(ADAPTER_RANK, 2 * KEYVALUE_HEADS, LANES)
        .transpose(1, 0, 2)
    )
    narrow_product, gathered = keyval(
        cube,
        cycle_size,
        moved,
        down_slice.reshape(D // cube, 3 * ADAPTER_RANK),
        keyval_up,
        key_base,
        value_base,
        cosine,
        sine,
    )
    gathered = gathered.reshape(cycle_size * tok_rows, -1)
    return attend(narrow_product, query_base, gathered, rest, cosine, sine)


def solution(mesh):
    placed = (
        P(("groups", "ctx"), None),
        P(("groups", "ctx"), None),
        P(("groups", "ctx"), None),
        P(("groups", "ctx"), None),
        P("ctx", None),
        P("groups"),
        P(),
    )
    return jax.shard_map(
        shards,
        mesh=mesh,
        in_specs=placed,
        out_specs=(P(("groups", "ctx"), None), P(("groups", "ctx"), None)),
        check_vma=False,
    )
```

time: 226 us -> 136 us (0.60)
  local copies, waits for them, and re-layouts: 74.9 us -> 6.67 us
  matrix products: 15.2 us -> 0 us
  other arithmetic: 8.9 us -> 1.86 us
    dynamic_slice x2 -> x0, local copies, waits for them, and re-layouts: 53.6 us -> none  [the longest x1 28.5 us: shards(): lax.dynamic_slice_in_dim(adapter_pool[0], group * (down_size // groups),...]
    slice x7 -> x0, local copies, waits for them, and re-layouts: 16.2 us -> none  [the longest x1 4.87 us: project_heads(): upper_part[ADAPTER_RANK * QH * HEAD_SIZE:]]
    dot_general x6 -> x0, matrix products: 15.2 us -> none  [the longest x1 6.55 us: online_update(): jnp.einsum('hqk,khd->hqd', weights.astype(jnp.bfloat16), value_slice, pre...]
    reduce_sum x1 -> x0, other arithmetic: 2.72 us -> none  [online_update(): new_sum = run_sum * rescale + jnp.sum(weights, axis=-1)]
    unnamed x15 -> x14, local copies, waits for them, and re-layouts: 0.58 us -> 3.16 us
  transfers between devices with their start and end apart: 1 -> 1, of which waited for: 0 -> 0; matrix products, arithmetic and copies ran while one was open for 25% -> 1% of each run, Pallas kernels for 0% -> 0%
where the time goes in v1:
time: 136 us
  Pallas kernels  121 us (89%)
  local copies, waits for them, and re-layouts  6.67 us (5%)
  between operations  3.43 us (3%)
  starting transfers between devices  3.05 us (2%)
  other arithmetic  1.86 us (1%)
    pallas_call x1, Pallas kernels, place_adapter(): pl.pallas_call(partial(place_adapter_kernel, groups, cubes, cube, down_si...  75.5 us
    pallas_call x1, Pallas kernels, keyval(): pl.pallas_call(partial(keyval_kernel, cube, count), out_shape=(jax.ShapeD...  29.9 us
    pallas_call x1, Pallas kernels, attend(): pl.pallas_call(partial(attend_kernel, math.gcd(kv.shape[0], 1024)), out_s...  15.2 us
    unnamed x14, local copies, waits for them, and re-layouts  3.16 us
    ppermute x1, starting transfers between devices, shards(): others.append(lax.ppermute(slots, 'groups', route))  3.05 us
  transfers between devices with their start and end apart: 1, of which 0 were waited for; matrix products, arithmetic and copies ran while one was open for 1% of the time, Pallas kernels for 0%

profile of v1, /device:TPU:0, one launch (start us, length us, event | category | flops | bytes accessed | tf_op | source)
XLA Modules:
  0.0 135.6 jit_solution(17697656348450658277)
XLA Ops:
  0.6 0.9 fusion.1
  1.5 3.1 %collective-permute-start = (s32[2]{0:T(128)S(1)}, s32[2]{0:T(128)S(1)}, u32[]{:S(2)}, u32[]{:S(2)}) collective-permute-start(s32[2]{0:T(128)S(1)} %fusion.1), channel_id=1, source_target_pairs={{0,16},{16,0},{1,17},{17,1},{2,18},{18,2},{3,19},{19,3},{4,20},{20... | collective-permute-start | bytes 32 | tf_op jit(solution)/shard_map/ppermute | solution.py:478
  4.5 0.6 dynamic_slice.4
  7.8 0.2 fusion
  8.0 0.1 pad_maximum_fusion
  8.1 0.0 copy-start.2
  8.1 0.0 copy-start.3
  8.1 0.0 collective-permute-done
  8.2 0.6 gather_fusion
  8.7 0.1 broadcast_select_fusion
  8.8 0.1 select_n.52
  8.9 0.6 pad_add_fusion.1.pick_ref
  9.5 0.0 copy-start.4
  9.5 0.0 copy-start.5
  9.5 75.5 %shard_map.86 = (bf16[8,64,1024]{2,1,0:T(8,128)(2,1)}, bf16[2,768,128]{2,1,0:T(8,128)(2,1)}, bf16[2,8,544,128]{3,2,1,0:T(8,128)(2,1)}) custom-call(s32[6]{0:T(128)} %pad_add_fusion.1.pick_ref, bf16[64,8192]{1,0:T(8,128)(2,1)} %x_ref.1, bf16[1,2686976]{1,0:T(2,128)(2,1)} %pool_ref.1), custom_call_target="tpu_custom_call" | custom-call | tf_op jit(solution)/shard_map/pallas_call | solution.py:218
  85.0 0.9 slice_bitcast_fusion
  86.0 1.4 %reshape.56.w_ref = bf16[1024,192]{1,0:T(8,128)(2,1)S(1)} reshape(bf16[2,768,128]{2,1,0:T(8,128)(2,1)} %get-tuple-element.8) | data formatting | bytes 786432 | tf_op jit(solution)/shard_map/reshape | solution.py:511
  87.3 0.0 copy-done.2
  87.3 0.0 copy-done.3
  87.4 0.0 copy-done.4
  87.4 0.0 copy-done.5
  87.4 0.0 copy-start.1
  87.4 1.2 copy-done.1
  88.6 29.9 %shard_map.87 = (bf16[64,192]{1,0:T(8,128)(2,1)S(1)}, bf16[16,64,1024]{2,1,0:T(8,128)(2,1)S(1)}) custom-call(bf16[8,64,1024]{2,1,0:T(8,128)(2,1)S(1)} %copy-done.1, bf16[1024,192]{1,0:T(8,128)(2,1)S(1)} %reshape.56.w_ref, bf16[8,64,128]{2,1,0:T(8,128)(2,1)S(1)} %bitcast.13, bf16[64,512]{1,0:T(8,128)(2,1)S(1)} %copy-done.4, bf16[64,512]{1,0:T(8,128)(2,1)S(1)} %copy-done.5, ...), custom_call_target="tpu_custom_call" | custom-call | tf_op jit(solution)/shard_map/pallas_call | solution.py:327
  118.5 0.0 copy-start
  118.5 1.3 copy-done
  119.9 0.0 copy-start.6
  119.9 0.6 copy-done.6
  120.5 15.2 %shard_map.88 = (bf16[64,4096]{1,0:T(8,128)(2,1)}, bf16[64,8192]{1,0:T(8,128)(2,1)}) custom-call(bf16[64,192]{1,0:T(8,128)(2,1)} %copy-done.6, bf16[64,4096]{1,0:T(8,128)(2,1)} %query_ref.1, bf16[1024,1024]{1,0:T(8,128)(2,1)} %bitcast.12, bf16[8704,128]{1,0:T(8,128)(2,1)} %bitcast.15, f32[64,128]{1,0:T(8,128)} %copy-done.2, f32[64,128]{1,0:T(8,128)} %copy-done.3), custom_call_target="tpu_custom_call" | custom-call | tf_op jit(solution)/shard_map/pallas_call | solution.py:439
  (9 shorter events, 0.1 us)
Async XLA Ops:
  1.5 6.7 %collective-permute-start = (s32[2]{0:T(128)S(1)}, s32[2]{0:T(128)S(1)}, u32[]{:S(2)}, u32[]{:S(2)}) collective-permute-start(s32[2]{0:T(128)S(1)} %fusion.1), channel_id=1, source_target_pairs={{0,16},{16,0},{1,17},{17,1},{2,18},{18,2},{3,19},{19,3},{4,20},{20... | collective-permute-start | bytes 32 | tf_op jit(solution)/shard_map/ppermute | solution.py:478
  8.1 79.2 %copy-start.2 = (f32[64,128]{1,0:T(8,128)}, f32[64,128]{1,0:T(8,128)S(1)}, u32[]{:S(2)}) copy-start(f32[64,128]{1,0:T(8,128)S(1)} %get-tuple-element.15.cos_ref) | copy-start | bytes 98308
  8.1 79.2 %copy-start.3 = (f32[64,128]{1,0:T(8,128)}, f32[64,128]{1,0:T(8,128)S(1)}, u32[]{:S(2)}) copy-start(f32[64,128]{1,0:T(8,128)S(1)} %get-tuple-element.16.sin_ref) | copy-start | bytes 98308
  9.5 77.9 %copy-start.4 = (bf16[64,512]{1,0:T(8,128)(2,1)S(1)}, bf16[64,512]{1,0:T(8,128)(2,1)}, u32[]{:S(2)}) copy-start(bf16[64,512]{1,0:T(8,128)(2,1)} %key_ref.1) | copy-start | bytes 196612
  9.5 77.9 %copy-start.5 = (bf16[64,512]{1,0:T(8,128)(2,1)S(1)}, bf16[64,512]{1,0:T(8,128)(2,1)}, u32[]{:S(2)}) copy-start(bf16[64,512]{1,0:T(8,128)(2,1)} %value_ref.1) | copy-start | bytes 196612
  87.4 1.2 copy-start.1
  118.5 1.3 copy-start
  119.9 0.6 copy-start.6

commit v2 on v1

--- a/solution.py
+++ b/solution.py
@@ -41,11 +41,12 @@
 
 def place_adapter_kernel(
     groups, cubes, cube, down_size,
-    pick_ref, x_ref, pool_ref,
+    owner_ref, stretch_ref, x_ref, pool_ref,
     x_out, down_out, rest_out,
     down_flat, rest_flat, down_source, rest_source,
     down_rows, rest_rows, down_send, rest_send, down_land, rest_land,
-    s_flat, s_cube, r_cube, s_far, r_far, s_tree, r_tree, s_own,
+    stretch_land, table,
+    s_flat, s_cube, r_cube, s_far, r_far, s_tree, r_tree, s_own, s_row, r_row, s_table,
 ):
     group = lax.axis_index("groups")
     ctx = lax.axis_index("ctx")
@@ -84,6 +85,13 @@
             device_id_type=MESH,
         )
     pl.semaphore_wait(barrier, cube - 1 + kinds - 1)
+    row_copies = []
+    for step in range(1, groups):
+        copy = remote(
+            stretch_ref, stretch_land.at[step], s_row.at[step], r_row.at[step], group ^ step, ctx
+        )
+        copy.start()
+        row_copies.append(copy)
 
     def columns(part, owner):
         return pl.ds(pl.multiple_of((part * cube + owner) * width, width), width)
@@ -120,6 +128,22 @@
         lax.fori_loop(0, cube - 1, spread, 0)
         read_piece(row, 0).wait()
         rows[inner] = dense(row, 0)
+
+    to_table = [pltpu.make_async_copy(stretch_ref, table.at[0], s_table.at[0])]
+    to_table[0].start()
+    for step, copy in zip(range(1, groups), row_copies):
+        copy.wait_recv()
+        move = pltpu.make_async_copy(stretch_land.at[step], table.at[step], s_table.at[step])
+        move.start()
+        to_table.append(move)
+    for move in to_table:
+        move.wait()
+
+    def slot_of(k):
+        return owner_ref[table[k // cubes, 0, outer ^ (k % cubes)]]
+
+    def chosen(part):
+        return (part * cubes + lax.div(slot_of(0), cube)) ^ home
 
     owns = []
     for part in range(groups):
@@ -140,20 +164,20 @@
         coming = []
         for k in range(1, kinds):
             there = home ^ k
-            outgoing[k] = rows[pick_ref[there]]
+            outgoing[k] = rows[lax.rem(slot_of(k), cube)]
             copy = remote(
                 outgoing.at[k], landing.at[k], s_far.at[row, k], r_far.at[row, k],
                 there // cubes, (there % cubes) * cube + inner,
             )
             copy.start()
             coming.append(copy)
-        landing[0] = rows[pick_ref[home]]
+        landing[0] = rows[lax.rem(slot_of(0), cube)]
         far.append(coming)
 
     for copy in far[0]:
         copy.wait_recv()
     for part in range(groups):
-        rest_out[part, inner] = rest_land[pick_ref[kinds + part]]
+        rest_out[part, inner] = rest_land[chosen(part)]
     tree = {}
     have = [[0] for _ in range(groups)]
     levels = cube.bit_length() - 1
@@ -189,7 +213,7 @@
     for copy in far[1]:
         copy.wait_recv()
     for part in range(groups):
-        down_out[part] = down_land[pick_ref[kinds + part]]
+        down_out[part] = down_land[chosen(part)]
     for (k, part), copy in tree.items():
         if k & orders[part][-1]:
             copy.wait_recv()
@@ -202,11 +226,11 @@
     for row in range(2):
         for k in range(1, cube):
             cube_copy(row, k).wait_send()
-    for copy in far[0] + far[1] + list(tree.values()):
+    for copy in row_copies + far[0] + far[1] + list(tree.values()):
         copy.wait_send()
 
 
-def place_adapter(groups, cubes, cube, down_size, picks, x, pool):
+def place_adapter(groups, cubes, cube, down_size, owner, stretch_row, x, pool):
     kinds = groups * cubes
     tokens, depth = x.shape
     down_piece = down_size // (groups * cube)
@@ -222,7 +246,7 @@
             jax.ShapeDtypeStruct((groups,) + down_shape, bf16),
             jax.ShapeDtypeStruct((groups, cube) + rest_shape, bf16),
         ),
-        in_specs=[SCALARS, ON_CHIP, pl.BlockSpec(memory_space=pl.ANY)],
+        in_specs=[SCALARS, ON_CHIP, ON_CHIP, pl.BlockSpec(memory_space=pl.ANY)],
         out_specs=(ON_CHIP, ON_CHIP, ON_CHIP),
         scratch_shapes=[
             pltpu.VMEM((cube, 1, down_piece), bf16),
@@ -235,6 +259,8 @@
             pltpu.VMEM((kinds,) + rest_shape, bf16),
             pltpu.VMEM((kinds,) + down_shape, bf16),
             pltpu.VMEM((kinds,) + rest_shape, bf16),
+            pltpu.VMEM((groups,) + stretch_row.shape, jnp.int32),
+            pltpu.SMEM((groups,) + stretch_row.shape, jnp.int32),
             dma((2, cube)),
             dma((2 + groups, cube)),
             dma((2 + groups, cube)),
@@ -243,18 +269,21 @@
             dma((groups, cube)),
             dma((groups, cube)),
             dma((groups,)),
+            dma((groups,)),
+            dma((groups,)),
+            dma((groups,)),
         ],
         compiler_params=pltpu.CompilerParams(
             collective_id=0, has_side_effects=True, vmem_limit_bytes=60 * 1024 * 1024
         ),
-    )(picks, x, pool)
+    )(owner, stretch_row, x, pool)
 
 
 def keyval_kernel(
     cube, count,
-    x_ref, w_ref, up_ref, key_ref, value_ref, cos_ref, sin_ref,
-    narrow_out, out_ref,
-    total, outgoing, landing, s_sem, r_sem, s_all, r_all,
+    x_ref, w_ref, up_ref, query_ref, key_ref, value_ref, cos_ref, sin_ref,
+    query_out, out_ref,
+    wide, total, outgoing, landing, s_sem, r_sem, s_all, r_all,
 ):
     group = lax.axis_index("groups")
     ctx = lax.axis_index("ctx")
@@ -280,17 +309,21 @@
         )
         copy.start()
         copies.append(copy)
+    wide[...] = up_ref[: wide.shape[0], :].astype(jnp.float32)
     result = total[inner]
     for k, copy in zip(range(1, cube), copies):
         copy.wait_recv()
         result = result + landing[k].astype(jnp.float32)
     low = result.astype(jnp.bfloat16)
-    narrow_out[...] = low
     half = HEAD_SIZE // 2
+    query_rows = ADAPTER_RANK * QH
+    kinds = 2 * KEYVALUE_HEADS
     for j in range(2 * KEYVALUE_HEADS):
         first = ADAPTER_RANK * (1 if j < KEYVALUE_HEADS else 2)
         delta = adapter_scale * jnp.dot(
-            low[:, first : first + ADAPTER_RANK], up_ref[j], preferred_element_type=jnp.float32
+            low[:, first : first + ADAPTER_RANK],
+            wide[pl.ds(query_rows + j, ADAPTER_RANK, stride=kinds), :].astype(jnp.bfloat16),
+            preferred_element_type=jnp.float32
         )
         base_ref = key_ref if j < KEYVALUE_HEADS else value_ref
         head = j % KEYVALUE_HEADS
@@ -299,62 +332,92 @@
             delta = delta * cos_ref[...] + swapped * sin_ref[...]
         base = base_ref[:, head * HEAD_SIZE : (head + 1) * HEAD_SIZE].astype(jnp.float32)
         out_ref[ctx, :, j * HEAD_SIZE : (j + 1) * HEAD_SIZE] = (base + delta).astype(jnp.bfloat16)
-    have = [0]
+
+    def query_head(head):
+        up = wide[pl.ds(head, ADAPTER_RANK, stride=QH), :].astype(jnp.bfloat16)
+        delta = adapter_scale * jnp.dot(
+            low[:, :ADAPTER_RANK], up, preferred_element_type=jnp.float32
+        )
+        swapped = jnp.concatenate([delta[:, half:], delta[:, :half]], axis=1)
+        delta = delta * cos_ref[...] + swapped * sin_ref[...]
+        base = query_ref[:, head * HEAD_SIZE : (head + 1) * HEAD_SIZE].astype(jnp.float32)
+        shared = QH // KEYVALUE_HEADS
+        query_out[
+            head // shared, (head % shared) * tokens : (head % shared + 1) * tokens, :
+        ] = (base + delta).astype(jnp.bfloat16)
+
+    kv_width = KEYVALUE_HEADS * HEAD_SIZE
+    far_first = [1 << level for level in reversed(range(levels))]
+    orders = (far_first, [2] + [bit for bit in far_first if bit != 2])
+    have = [[0], [0]]
     moved = {}
-    for level in reversed(range(levels)):
-        bit = 1 << level
-        new = []
-        for k in have:
-            if k & (bit << 1):
-                moved[k].wait_recv()
-            slot = out_ref.at[ctx ^ k]
-            copy = remote(slot, slot, s_all.at[k ^ bit], r_all.at[k ^ bit], group, ctx ^ bit)
-            copy.start()
-            moved[k ^ bit] = copy
-            new.append(k ^ bit)
-        have = have + new
-    for k, copy in moved.items():
-        if k & 1:
+    done = 0
+    for stage in range(levels):
+        for part in range(2):
+            bit = orders[part][stage]
+            before = orders[part][stage - 1] if stage else 0
+            new = []
+            for k in have[part]:
+                if k & before:
+                    moved[k, part].wait_recv()
+                slot = out_ref.at[ctx ^ k, :, pl.ds(part * kv_width, kv_width)]
+                copy = remote(
+                    slot, slot, s_all.at[part, k ^ bit], r_all.at[part, k ^ bit], group, ctx ^ bit
+                )
+                copy.start()
+                moved[k ^ bit, part] = copy
+                new.append(k ^ bit)
+            have[part] = have[part] + new
+        until = QH * (stage + 1) // levels
+        for head in range(done, until):
+            query_head(head)
+        done = until
+    for (k, part), copy in moved.items():
+        if k & orders[part][-1]:
             copy.wait_recv()
     for copy in copies + list(moved.values()):
         copy.wait_send()
 
 
-def keyval(cube, count, x, w, up, key_rows, value_rows, cosine, sine):
+def keyval(cube, count, x, w, rest, query_rows, key_rows, value_rows, cosine, sine):
     _, tokens, _ = x.shape
     shape = (cube, tokens, w.shape[1])
+    up_rows = ADAPTER_RANK * (QH + 2 * KEYVALUE_HEADS)
     dma = pltpu.SemaphoreType.DMA
     return pl.pallas_call(
         partial(keyval_kernel, cube, count),
         out_shape=(
-            jax.ShapeDtypeStruct(shape[1:], jnp.bfloat16),
+            jax.ShapeDtypeStruct(
+                (KEYVALUE_HEADS, QH // KEYVALUE_HEADS * tokens, HEAD_SIZE), jnp.bfloat16
+            ),
             jax.ShapeDtypeStruct(
                 (count, tokens, 2 * KEYVALUE_HEADS * HEAD_SIZE), jnp.bfloat16
             ),
         ),
-        in_specs=[ON_CHIP] * 7,
+        in_specs=[ON_CHIP] * 8,
         out_specs=(ON_CHIP, ON_CHIP),
         scratch_shapes=[
+            pltpu.VMEM((up_rows, LANES), jnp.float32),
             pltpu.VMEM(shape, jnp.float32),
             pltpu.VMEM(shape, jnp.bfloat16),
             pltpu.VMEM(shape, jnp.bfloat16),
             dma((cube,)),
             dma((cube,)),
-            dma((count,)),
-            dma((count,)),
+            dma((2, count)),
+            dma((2, count)),
         ],
         compiler_params=pltpu.CompilerParams(
             collective_id=1, has_side_effects=True, vmem_limit_bytes=40 * 1024 * 1024
         ),
-    )(x, w, up, key_rows, value_rows, cosine, sine)
+    )(x, w, rest, query_rows, key_rows, value_rows, cosine, sine)
 
 
 def attend_kernel(
-    step_keys, narrow_ref, query_ref, kv_ref, rest_ref, cos_ref, sin_ref,
+    step_keys, queries, kv_ref, rest_ref,
     attended_ref, delta_ref,
-    wide, queries, permuted, run_max, run_sum, run_acc,
+    wide, permuted, run_max, run_sum, run_acc,
 ):
-    tokens = narrow_ref.shape[0]
+    tokens = attended_ref.shape[0]
     ctx = lax.axis_index("ctx")
     heads = QH // KEYVALUE_HEADS
     rows = heads * tokens
@@ -362,16 +425,7 @@
     query_rows = ADAPTER_RANK * QH
     out_start = query_rows + 2 * ADAPTER_RANK * KEYVALUE_HEADS
     raise_start = out_start + QH * half
-    wide[...] = rest_ref[...].astype(jnp.float32)
-    low = narrow_ref[:, :ADAPTER_RANK]
-    for head in range(QH):
-        up = wide[pl.ds(head, ADAPTER_RANK, stride=QH), :].astype(jnp.bfloat16)
-        delta = adapter_scale * jnp.dot(low, up, preferred_element_type=jnp.float32)
-        delta = delta * cos_ref[...] + pltpu.roll(delta, half, 1) * sin_ref[...]
-        base = query_ref[:, head * HEAD_SIZE : (head + 1) * HEAD_SIZE].astype(jnp.float32)
-        queries[head // heads, pl.ds((head % heads) * tokens, tokens), :] = (base + delta).astype(
-            jnp.bfloat16
-        )
+    wide[...] = rest_ref[raise_start:, :].astype(jnp.float32)
     first = ctx * tokens
     steps = (first + tokens + step_keys - 1) // step_keys
     row = lax.broadcasted_iota(jnp.int32, (rows, step_keys), 0)
@@ -427,33 +481,32 @@
     narrow = narrow.astype(jnp.bfloat16)
     blocks = D // LANES
     for j in range(blocks):
-        up = wide[pl.ds(raise_start + j, ADAPTER_RANK, stride=blocks), :].astype(jnp.bfloat16)
+        up = wide[pl.ds(j, ADAPTER_RANK, stride=blocks), :].astype(jnp.bfloat16)
         delta_ref[:, j * LANES : (j + 1) * LANES] = (
             adapter_scale * jnp.dot(narrow, up, preferred_element_type=jnp.float32)
         ).astype(jnp.bfloat16)
 
 
-def attend(narrow, query_rows, kv, rest, cosine, sine):
-    tokens = narrow.shape[0]
-    rows = QH // KEYVALUE_HEADS * tokens
+def attend(queries, kv, rest):
+    rows = queries.shape[1]
+    tokens = rows // (QH // KEYVALUE_HEADS)
     return pl.pallas_call(
         partial(attend_kernel, math.gcd(kv.shape[0], 1024)),
         out_shape=(
             jax.ShapeDtypeStruct((tokens, QH * HEAD_SIZE), jnp.bfloat16),
             jax.ShapeDtypeStruct((tokens, D), jnp.bfloat16),
         ),
-        in_specs=[ON_CHIP] * 6,
+        in_specs=[ON_CHIP] * 3,
         out_specs=(ON_CHIP, ON_CHIP),
         scratch_shapes=[
-            pltpu.VMEM(rest.shape, jnp.float32),
-            pltpu.VMEM((KEYVALUE_HEADS, rows, HEAD_SIZE), jnp.bfloat16),
+            pltpu.VMEM((ADAPTER_RANK * D // LANES, LANES), jnp.float32),
             pltpu.VMEM((tokens, QH * HEAD_SIZE), jnp.bfloat16),
             pltpu.VMEM((rows, 1), jnp.float32),
             pltpu.VMEM((rows, 1), jnp.float32),
             pltpu.VMEM((rows, HEAD_SIZE), jnp.float32),
         ],
         compiler_params=pltpu.CompilerParams(vmem_limit_bytes=56 * 1024 * 1024),
-    )(narrow, query_rows, kv, rest, cosine, sine)
+    )(queries, kv, rest)
 
 
 def shards(
@@ -464,28 +517,10 @@
     tok_rows = normed_input.shape[0]
     token_positions = my_index * tok_rows + jnp.arange(tok_rows, dtype=jnp.int32)
     groups = lax.axis_size("groups")
-    group = lax.axis_index("groups")
     cube = BLOCK_TOKENS // tok_rows
     cubes = cycle_size // cube
-    adapter_ids = jnp.arange(adapter_owner.shape[0], dtype=jnp.int32)
-    slots = jnp.sum(
-        jnp.where(stretch_adapter[:, None] == adapter_ids[None, :], adapter_owner[None, :], 0),
-        axis=1,
-    )
-    others = [slots]
-    for step in range(1, groups):
-        route = [(low, low ^ step) for low in range(groups)]
-        others.append(lax.ppermute(slots, "groups", route))
-    by_step = jnp.stack(others)
-    all_slots = jnp.take(
-        by_step, jnp.bitwise_xor(group, jnp.arange(groups, dtype=jnp.int32)), axis=0
-    )
-    my_slot = lax.dynamic_index_in_dim(slots, my_index // cube, 0, keepdims=False)
-    home = group * cubes + my_index // cube
-    chosen = jnp.bitwise_xor(
-        jnp.arange(groups, dtype=jnp.int32) * cubes + my_slot // cube, home
-    )
-    picks = jnp.concatenate([(all_slots % cube).reshape(-1), chosen]).astype(jnp.int32)
+    padding = -stretch_adapter.shape[0] % LANES
+    stretch_row = jnp.pad(stretch_adapter, (0, padding))[None]
     down_size = 3 * ADAPTER_RANK * D
     half_dim = HEAD_SIZE // 2
     frequency = rope_base ** (-(jnp.arange(half_dim, dtype=jnp.float32) * 2.0) / HEAD_SIZE)
@@ -495,28 +530,23 @@
     cosine = jnp.concatenate([cosine, cosine], axis=1)
     sine = jnp.concatenate([-sine, sine], axis=1)
     moved, down_slice, rest = place_adapter(
-        groups, cubes, cube, down_size, picks, normed_input, adapter_pool
+        groups, cubes, cube, down_size, adapter_owner, stretch_row, normed_input, adapter_pool
     )
     rest = rest.reshape(-1, LANES)
-    query_part = ADAPTER_RANK * QH
-    keyval_up = (
-        rest[query_part : query_part + 2 * ADAPTER_RANK * KEYVALUE_HEADS]
-        .reshape(ADAPTER_RANK, 2 * KEYVALUE_HEADS, LANES)
-        .transpose(1, 0, 2)
-    )
-    narrow_product, gathered = keyval(
+    queries, gathered = keyval(
         cube,
         cycle_size,
         moved,
         down_slice.reshape(D // cube, 3 * ADAPTER_RANK),
-        keyval_up,
+        rest,
+        query_base,
         key_base,
         value_base,
         cosine,
         sine,
     )
     gathered = gathered.reshape(cycle_size * tok_rows, -1)
-    return attend(narrow_product, query_base, gathered, rest, cosine, sine)
+    return attend(queries, gathered, rest)
 
 
 def solution(mesh):

time: 136 us -> 125 us (0.919)
  Pallas kernels: 121 us -> 116 us
  starting transfers between devices: 3.05 us -> 0 us
  between operations: 3.43 us -> 0.75 us
  other arithmetic: 1.86 us -> 0.3 us
    pallas_call x1, Pallas kernels: 29.9 us -> 25.1 us  [keyval(): pl.pallas_call(partial(keyval_kernel, cube, count), out_shape=(jax.ShapeD...]
    ppermute x1 -> x0, starting transfers between devices: 3.05 us -> none  [shards(): others.append(lax.ppermute(slots, 'groups', route))]
    unnamed x14, local copies, waits for them, and re-layouts: 3.16 us -> 4.98 us
    pallas_call x1, Pallas kernels: 75.5 us -> 77.1 us  [place_adapter(): pl.pallas_call(partial(place_adapter_kernel, groups, cubes, cube, down_si...]
  transfers between devices with their start and end apart: 1 -> 0, of which waited for: 0 -> 0; matrix products, arithmetic and copies ran while one was open for 1% -> 0% of each run, Pallas kernels for 0% -> 0%
where the time goes in v2:
time: 125 us
  Pallas kernels  116 us (93%)
  local copies, waits for them, and re-layouts  7.51 us (6%)
    pallas_call x1, Pallas kernels, place_adapter(): pl.pallas_call(partial(place_adapter_kernel, groups, cubes, cube, down_si...  77.1 us
    pallas_call x1, Pallas kernels, keyval(): pl.pallas_call(partial(keyval_kernel, cube, count), out_shape=(jax.ShapeD...  25.1 us
    pallas_call x1, Pallas kernels, attend(): pl.pallas_call(partial(attend_kernel, math.gcd(kv.shape[0], 1024)), out_s...  14.1 us
    unnamed x14, local copies, waits for them, and re-layouts  4.98 us

profile of v2, /device:TPU:0, one launch (start us, length us, event | category | flops | bytes accessed | tf_op | source)
XLA Modules:
  0.0 124.9 jit_solution(4293595062664790220)
XLA Ops:
  0.6 1.2 pad_bitcast_fusion.stretch_ref
  1.8 0.2 fusion
  2.0 0.1 pad_maximum_fusion
  2.1 0.0 copy-start.3
  2.1 0.0 copy-start.5
  2.1 0.0 copy-start.6
  2.2 77.1 %shard_map.86 = (bf16[8,64,1024]{2,1,0:T(8,128)(2,1)}, bf16[2,768,128]{2,1,0:T(8,128)(2,1)}, bf16[2,8,544,128]{3,2,1,0:T(8,128)(2,1)}) custom-call(s32[16]{0:T(128)} %owner_ref.1, s32[1,128]{1,0:T(1,128)} %pad_bitcast_fusion.stretch_ref, bf16[64,8192]{1,0:T(8,128)(2,1)} %x_ref.1, bf16[1,2686976]{1,0:T(2,128)(2,1)} %pool_ref.1), custom_call_target="tpu_custom_call" | custom-call | tf_op jit(solution)/shard_map/pallas_call | solution.py:242
  79.2 1.4 %reshape.25.w_ref = bf16[1024,192]{1,0:T(8,128)(2,1)S(1)} reshape(bf16[2,768,128]{2,1,0:T(8,128)(2,1)} %get-tuple-element.8) | data formatting | bytes 786432 | tf_op jit(solution)/shard_map/reshape | solution.py:540
  80.6 0.0 copy-done.3
  80.6 0.0 copy-done.5
  80.6 0.0 copy-done.6
  80.6 0.0 copy-start
  80.6 1.6 %copy-done = bf16[2,8,544,128]{3,2,1,0:T(8,128)(2,1)S(1)} copy-done((bf16[2,8,544,128]{3,2,1,0:T(8,128)(2,1)S(1)}, bf16[2,8,544,128]{3,2,1,0:T(8,128)(2,1)}, u32[]{:S(2)}) %copy-start) | copy-done | bytes 2228248
  82.3 0.0 copy-start.2
  82.3 1.2 copy-done.2
  83.5 25.1 %shard_map.87 = (bf16[4,512,128]{2,1,0:T(8,128)(2,1)S(1)}, bf16[16,64,1024]{2,1,0:T(8,128)(2,1)S(1)}) custom-call(bf16[8,64,1024]{2,1,0:T(8,128)(2,1)S(1)} %copy-done.2, bf16[1024,192]{1,0:T(8,128)(2,1)S(1)} %reshape.25.w_ref, bf16[8704,128]{1,0:T(8,128)(2,1)S(1)} %bitcast.5, bf16[64,4096]{1,0:T(8,128)(2,1)S(1)} %copy-done.3, bf16[64,512]{1,0:T(8,128)(2,1)S(1)} %copy-done.5, ...), custom_call_target="tpu_custom_call" | custom-call | tf_op jit(solution)/shard_map/pallas_call | solution.py:387
  108.6 0.0 copy-start.1
  108.6 1.3 %copy-done.1 = bf16[16,64,1024]{2,1,0:T(8,128)(2,1)} copy-done((bf16[16,64,1024]{2,1,0:T(8,128)(2,1)}, bf16[16,64,1024]{2,1,0:T(8,128)(2,1)S(1)}, u32[]{:S(2)}) %copy-start.1) | copy-done | bytes 2097176
  109.9 0.0 copy-start.4
  109.9 0.8 copy-done.4
  110.7 14.1 %shard_map.88 = (bf16[64,4096]{1,0:T(8,128)(2,1)}, bf16[64,8192]{1,0:T(8,128)(2,1)}) custom-call(bf16[4,512,128]{2,1,0:T(8,128)(2,1)} %copy-done.4, bf16[1024,1024]{1,0:T(8,128)(2,1)} %bitcast.6, bf16[8704,128]{1,0:T(8,128)(2,1)} %bitcast.4), custom_call_target="tpu_custom_call" | custom-call | tf_op jit(solution)/shard_map/pallas_call | solution.py:493
  (2 shorter events, 0.0 us)
Async XLA Ops:
  2.1 78.5 %copy-start.3 = (bf16[64,4096]{1,0:T(8,128)(2,1)S(1)}, bf16[64,4096]{1,0:T(8,128)(2,1)}, u32[]{:S(2)}) copy-start(bf16[64,4096]{1,0:T(8,128)(2,1)} %query_ref.1) | copy-start | bytes 1572868
  2.1 78.5 %copy-start.5 = (bf16[64,512]{1,0:T(8,128)(2,1)S(1)}, bf16[64,512]{1,0:T(8,128)(2,1)}, u32[]{:S(2)}) copy-start(bf16[64,512]{1,0:T(8,128)(2,1)} %key_ref.1) | copy-start | bytes 196612
  2.1 78.5 %copy-start.6 = (bf16[64,512]{1,0:T(8,128)(2,1)S(1)}, bf16[64,512]{1,0:T(8,128)(2,1)}, u32[]{:S(2)}) copy-start(bf16[64,512]{1,0:T(8,128)(2,1)} %value_ref.1) | copy-start | bytes 196612
  80.6 1.6 %copy-start = (bf16[2,8,544,128]{3,2,1,0:T(8,128)(2,1)S(1)}, bf16[2,8,544,128]{3,2,1,0:T(8,128)(2,1)}, u32[]{:S(2)}) copy-start(bf16[2,8,544,128]{3,2,1,0:T(8,128)(2,1)} %get-tuple-element.9) | copy-start | bytes 6684676
  82.3 1.2 copy-start.2
  108.6 1.3 %copy-start.1 = (bf16[16,64,1024]{2,1,0:T(8,128)(2,1)}, bf16[16,64,1024]{2,1,0:T(8,128)(2,1)S(1)}, u32[]{:S(2)}) copy-start(bf16[16,64,1024]{2,1,0:T(8,128)(2,1)S(1)} %get-tuple-element.11) | copy-start | bytes 6291460
  109.9 0.8 copy-start.4

commit v3 on v2

--- a/solution.py
+++ b/solution.py
@@ -25,6 +25,7 @@
 LANES = 128
 MESH = pl.DeviceIdType.MESH
 ON_CHIP = pl.BlockSpec(memory_space=pltpu.VMEM)
+ANYWHERE = pl.BlockSpec(memory_space=pl.ANY)
 SCALARS = pl.BlockSpec(memory_space=pltpu.SMEM)
 
 
@@ -281,20 +282,27 @@
 
 def keyval_kernel(
     cube, count,
-    x_ref, w_ref, up_ref, query_ref, key_ref, value_ref, cos_ref, sin_ref,
+    x_any, w_ref, rest_any, query_ref, key_ref, value_ref, cos_ref, sin_ref,
     query_out, out_ref,
-    wide, total, outgoing, landing, s_sem, r_sem, s_all, r_all,
+    x_ref, up_ref, s_in, wide, total, outgoing, landing, s_sem, r_sem, s_all, r_all,
 ):
     group = lax.axis_index("groups")
     ctx = lax.axis_index("ctx")
     inner = ctx % cube
     outer = ctx // cube
     levels = count.bit_length() - 1
+    x_in = pltpu.make_async_copy(x_any, x_ref, s_in.at[0])
+    x_in.start()
+    up_in = pltpu.make_async_copy(
+        rest_any.at[pl.ds(0, up_ref.shape[0])], up_ref, s_in.at[1]
+    )
+    up_in.start()
     barrier = pltpu.get_barrier_semaphore()
     apart = list(range(1, cube)) + [1 << n for n in range(levels) if 1 << n >= cube]
     for k in apart:
         pl.semaphore_signal(barrier, inc=1, device_id=(group, ctx ^ k), device_id_type=MESH)
     _, tokens, depth = x_ref.shape
+    x_in.wait()
     product = jnp.dot(
         x_ref[...].reshape(cube * tokens, depth), w_ref[...], preferred_element_type=jnp.float32
     ).reshape(cube, tokens, w_ref.shape[1])
@@ -309,7 +317,8 @@
         )
         copy.start()
         copies.append(copy)
-    wide[...] = up_ref[: wide.shape[0], :].astype(jnp.float32)
+    up_in.wait()
+    wide[...] = up_ref[...].astype(jnp.float32)
     result = total[inner]
     for k, copy in zip(range(1, cube), copies):
         copy.wait_recv()
@@ -394,9 +403,12 @@
                 (count, tokens, 2 * KEYVALUE_HEADS * HEAD_SIZE), jnp.bfloat16
             ),
         ),
-        in_specs=[ON_CHIP] * 8,
+        in_specs=[ANYWHERE, ON_CHIP, ANYWHERE] + [ON_CHIP] * 5,
         out_specs=(ON_CHIP, ON_CHIP),
         scratch_shapes=[
+            pltpu.VMEM(x.shape, jnp.bfloat16),
+            pltpu.VMEM((up_rows, LANES), jnp.bfloat16),
+            dma((2,)),
             pltpu.VMEM((up_rows, LANES), jnp.float32),
             pltpu.VMEM(shape, jnp.float32),
             pltpu.VMEM(shape, jnp.bfloat16),
@@ -413,9 +425,9 @@
 
 
 def attend_kernel(
-    step_keys, queries, kv_ref, rest_ref,
+    step_keys, queries, kv_ref, rest_any,
     attended_ref, delta_ref,
-    wide, permuted, run_max, run_sum, run_acc,
+    rest_ref, s_in, wide, permuted, run_max, run_sum, run_acc,
 ):
     tokens = attended_ref.shape[0]
     ctx = lax.axis_index("ctx")
@@ -423,9 +435,13 @@
     rows = heads * tokens
     half = HEAD_SIZE // 2
     query_rows = ADAPTER_RANK * QH
-    out_start = query_rows + 2 * ADAPTER_RANK * KEYVALUE_HEADS
-    raise_start = out_start + QH * half
-    wide[...] = rest_ref[raise_start:, :].astype(jnp.float32)
+    raise_start = QH * half
+    rest_in = pltpu.make_async_copy(
+        rest_any.at[pl.ds(query_rows + 2 * ADAPTER_RANK * KEYVALUE_HEADS, rest_ref.shape[0])],
+        rest_ref,
+        s_in,
+    )
+    rest_in.start()
     first = ctx * tokens
     steps = (first + tokens + step_keys - 1) // step_keys
     row = lax.broadcasted_iota(jnp.int32, (rows, step_keys), 0)
@@ -469,9 +485,11 @@
             cols = slice(head * HEAD_SIZE, (head + 1) * HEAD_SIZE)
             attended_ref[:, cols] = result[j * tokens : (j + 1) * tokens]
             permuted[:, cols] = mixed[j * tokens : (j + 1) * tokens]
+    rest_in.wait()
+    wide[...] = rest_ref[raise_start:, :].astype(jnp.float32)
     narrow = jnp.zeros((tokens, ADAPTER_RANK), jnp.float32)
     for head in range(QH):
-        block = rest_ref[out_start + head * half : out_start + (head + 1) * half, :]
+        block = rest_ref[head * half : (head + 1) * half, :]
         weight = jnp.concatenate([block[:, :half], block[:, half:]], axis=0)
         narrow = narrow + jnp.dot(
             permuted[:, head * HEAD_SIZE : (head + 1) * HEAD_SIZE],
@@ -490,15 +508,18 @@
 def attend(queries, kv, rest):
     rows = queries.shape[1]
     tokens = rows // (QH // KEYVALUE_HEADS)
+    out_rows = ADAPTER_RANK * (QH * HEAD_SIZE + D) // LANES
     return pl.pallas_call(
         partial(attend_kernel, math.gcd(kv.shape[0], 1024)),
         out_shape=(
             jax.ShapeDtypeStruct((tokens, QH * HEAD_SIZE), jnp.bfloat16),
             jax.ShapeDtypeStruct((tokens, D), jnp.bfloat16),
         ),
-        in_specs=[ON_CHIP] * 3,
+        in_specs=[ON_CHIP, ON_CHIP, ANYWHERE],
         out_specs=(ON_CHIP, ON_CHIP),
         scratch_shapes=[
+            pltpu.VMEM((out_rows, LANES), jnp.bfloat16),
+            pltpu.SemaphoreType.DMA,
             pltpu.VMEM((ADAPTER_RANK * D // LANES, LANES), jnp.float32),
             pltpu.VMEM((tokens, QH * HEAD_SIZE), jnp.bfloat16),
             pltpu.VMEM((rows, 1), jnp.float32),

time: 125 us -> 125 us (level)
  no operation moved by 1% of the time
where the time goes in v3:
time: 125 us
  Pallas kernels  116 us (93%)
  local copies, waits for them, and re-layouts  7.51 us (6%)
    pallas_call x1, Pallas kernels, place_adapter(): pl.pallas_call(partial(place_adapter_kernel, groups, cubes, cube, down_si...  77.1 us
    pallas_call x1, Pallas kernels, keyval(): pl.pallas_call(partial(keyval_kernel, cube, count), out_shape=(jax.ShapeD...  25.4 us
    pallas_call x1, Pallas kernels, attend(): pl.pallas_call(partial(attend_kernel, math.gcd(kv.shape[0], 1024)), out_s...  13.8 us
    unnamed x14, local copies, waits for them, and re-layouts  4.98 us

profile of v3, /device:TPU:0, one launch (start us, length us, event | category | flops | bytes accessed | tf_op | source)
XLA Modules:
  0.0 124.8 jit_solution(11603591149912443816)
XLA Ops:
  0.6 1.2 pad_bitcast_fusion.stretch_ref
  1.8 0.2 fusion
  2.0 0.1 pad_maximum_fusion
  2.1 0.0 copy-start.3
  2.1 0.0 copy-start.5
  2.1 0.0 copy-start.6
  2.2 77.1 %shard_map.86 = (bf16[8,64,1024]{2,1,0:T(8,128)(2,1)}, bf16[2,768,128]{2,1,0:T(8,128)(2,1)}, bf16[2,8,544,128]{3,2,1,0:T(8,128)(2,1)}) custom-call(s32[16]{0:T(128)} %owner_ref.1, s32[1,128]{1,0:T(1,128)} %pad_bitcast_fusion.stretch_ref, bf16[64,8192]{1,0:T(8,128)(2,1)} %x_ref.1, bf16[1,2686976]{1,0:T(2,128)(2,1)} %pool_ref.1), custom_call_target="tpu_custom_call" | custom-call | tf_op jit(solution)/shard_map/pallas_call | solution.py:243
  79.2 1.4 %reshape.25.w_ref = bf16[1024,192]{1,0:T(8,128)(2,1)S(1)} reshape(bf16[2,768,128]{2,1,0:T(8,128)(2,1)} %get-tuple-element.8) | data formatting | bytes 786432 | tf_op jit(solution)/shard_map/reshape | solution.py:561
  80.6 0.0 copy-done.3
  80.6 0.0 copy-done.5
  80.6 0.0 copy-done.6
  80.6 0.0 copy-start
  80.6 1.6 %copy-done = bf16[2,8,544,128]{3,2,1,0:T(8,128)(2,1)S(1)} copy-done((bf16[2,8,544,128]{3,2,1,0:T(8,128)(2,1)S(1)}, bf16[2,8,544,128]{3,2,1,0:T(8,128)(2,1)}, u32[]{:S(2)}) %copy-start) | copy-done | bytes 2228248
  82.3 0.0 copy-start.2
  82.3 1.2 copy-done.2
  83.5 25.4 %shard_map.87 = (bf16[4,512,128]{2,1,0:T(8,128)(2,1)S(1)}, bf16[16,64,1024]{2,1,0:T(8,128)(2,1)S(1)}) custom-call(bf16[8,64,1024]{2,1,0:T(8,128)(2,1)S(1)} %copy-done.2, bf16[1024,192]{1,0:T(8,128)(2,1)S(1)} %reshape.25.w_ref, bf16[8704,128]{1,0:T(8,128)(2,1)S(1)} %bitcast.5, bf16[64,4096]{1,0:T(8,128)(2,1)S(1)} %copy-done.3, bf16[64,512]{1,0:T(8,128)(2,1)S(1)} %copy-done.5, ...), custom_call_target="tpu_custom_call" | custom-call | tf_op jit(solution)/shard_map/pallas_call | solution.py:396
  108.9 0.0 copy-start.1
  108.9 1.3 %copy-done.1 = bf16[16,64,1024]{2,1,0:T(8,128)(2,1)} copy-done((bf16[16,64,1024]{2,1,0:T(8,128)(2,1)}, bf16[16,64,1024]{2,1,0:T(8,128)(2,1)S(1)}, u32[]{:S(2)}) %copy-start.1) | copy-done | bytes 2097176
  110.2 0.0 copy-start.4
  110.2 0.8 copy-done.4
  111.0 13.8 %shard_map.88 = (bf16[64,4096]{1,0:T(8,128)(2,1)}, bf16[64,8192]{1,0:T(8,128)(2,1)}) custom-call(bf16[4,512,128]{2,1,0:T(8,128)(2,1)} %copy-done.4, bf16[1024,1024]{1,0:T(8,128)(2,1)} %bitcast.6, bf16[8704,128]{1,0:T(8,128)(2,1)} %bitcast.4), custom_call_target="tpu_custom_call" | custom-call | tf_op jit(solution)/shard_map/pallas_call | solution.py:512
  (2 shorter events, 0.0 us)
Async XLA Ops:
  2.1 78.5 %copy-start.3 = (bf16[64,4096]{1,0:T(8,128)(2,1)S(1)}, bf16[64,4096]{1,0:T(8,128)(2,1)}, u32[]{:S(2)}) copy-start(bf16[64,4096]{1,0:T(8,128)(2,1)} %query_ref.1) | copy-start | bytes 1572868
  2.1 78.5 %copy-start.5 = (bf16[64,512]{1,0:T(8,128)(2,1)S(1)}, bf16[64,512]{1,0:T(8,128)(2,1)}, u32[]{:S(2)}) copy-start(bf16[64,512]{1,0:T(8,128)(2,1)} %key_ref.1) | copy-start | bytes 196612
  2.1 78.5 %copy-start.6 = (bf16[64,512]{1,0:T(8,128)(2,1)S(1)}, bf16[64,512]{1,0:T(8,128)(2,1)}, u32[]{:S(2)}) copy-start(bf16[64,512]{1,0:T(8,128)(2,1)} %value_ref.1) | copy-start | bytes 196612
  80.6 1.6 %copy-start = (bf16[2,8,544,128]{3,2,1,0:T(8,128)(2,1)S(1)}, bf16[2,8,544,128]{3,2,1,0:T(8,128)(2,1)}, u32[]{:S(2)}) copy-start(bf16[2,8,544,128]{3,2,1,0:T(8,128)(2,1)} %get-tuple-element.9) | copy-start | bytes 6684676
  82.3 1.2 copy-start.2
  108.9 1.3 %copy-start.1 = (bf16[16,64,1024]{2,1,0:T(8,128)(2,1)}, bf16[16,64,1024]{2,1,0:T(8,128)(2,1)S(1)}, u32[]{:S(2)}) copy-start(bf16[16,64,1024]{2,1,0:T(8,128)(2,1)S(1)} %get-tuple-element.11) | copy-start | bytes 6291460
  110.2 0.8 copy-start.4

commit v4 on v3

--- a/solution.py
+++ b/solution.py
@@ -275,7 +275,9 @@
             dma((groups,)),
         ],
         compiler_params=pltpu.CompilerParams(
-            collective_id=0, has_side_effects=True, vmem_limit_bytes=60 * 1024 * 1024
+            collective_id=0,
+            has_side_effects=True,
+            vmem_limit_bytes=22 * 1024 * 1024 + 4 * kinds * (down_piece + rest_piece),
         ),
     )(owner, stretch_row, x, pool)
 
@@ -419,7 +421,10 @@
             dma((2, count)),
         ],
         compiler_params=pltpu.CompilerParams(
-            collective_id=1, has_side_effects=True, vmem_limit_bytes=40 * 1024 * 1024
+            collective_id=1,
+            has_side_effects=True,
+            vmem_limit_bytes=16 * 1024 * 1024
+            + 4 * count * tokens * KEYVALUE_HEADS * HEAD_SIZE,
         ),
     )(x, w, rest, query_rows, key_rows, value_rows, cosine, sine)
 

time: 125 us -> 130 us (1.040)
  local copies, waits for them, and re-layouts: 7.51 us -> 13.2 us
    unnamed x14 -> x24, local copies, waits for them, and re-layouts: 4.98 us -> 11 us
where the time goes in v4:
time: 130 us
  Pallas kernels  115 us (88%)
  local copies, waits for them, and re-layouts  13.2 us (10%)
    pallas_call x1, Pallas kernels, place_adapter(): pl.pallas_call(partial(place_adapter_kernel, groups, cubes, cube, down_si...  76.3 us
    pallas_call x1, Pallas kernels, keyval(): pl.pallas_call(partial(keyval_kernel, cube, count), out_shape=(jax.ShapeD...  25.4 us
    pallas_call x1, Pallas kernels, attend(): pl.pallas_call(partial(attend_kernel, math.gcd(kv.shape[0], 1024)), out_s...  13.8 us
    unnamed x24, local copies, waits for them, and re-layouts  11 us

profile of v4, /device:TPU:0, one launch (start us, length us, event | category | flops | bytes accessed | tf_op | source)
XLA Modules:
  0.0 129.8 jit_solution(12866915432860456956)
XLA Ops:
  0.6 0.7 pad_bitcast_fusion.stretch_ref
  1.3 0.2 fusion
  1.5 0.1 pad_maximum_fusion
  1.6 0.0 copy-start
  1.6 4.0 %copy-done = bf16[1,2686976]{1,0:T(2,128)(2,1)S(1)} copy-done((bf16[1,2686976]{1,0:T(2,128)(2,1)S(1)}, bf16[1,2686976]{1,0:T(2,128)(2,1)}, u32[]{:S(2)}) %copy-start) | copy-done | bytes 5373976
  5.7 0.0 copy-start.3
  5.7 1.2 copy-done.3
  6.9 0.0 copy-start.11
  6.9 0.7 copy-done.11
  7.6 0.0 copy-start.6
  7.6 0.0 copy-start.9
  7.6 0.0 copy-start.10
  7.6 76.3 %shard_map.86 = (bf16[8,64,1024]{2,1,0:T(8,128)(2,1)S(1)}, bf16[2,768,128]{2,1,0:T(8,128)(2,1)S(1)}, bf16[2,8,544,128]{3,2,1,0:T(8,128)(2,1)S(1)}) custom-call(s32[16]{0:T(128)S(1)} %copy-done.11, s32[1,128]{1,0:T(1,128)S(1)} %pad_bitcast_fusion.stretch_ref, bf16[64,8192]{1,0:T(8,128)(2,1)S(1)} %copy-done.3, bf16[1,2686976]{1,0:T(2,128)(2,1)S(1)} %copy-done), custom_call_target="tpu_custom_call" | custom-call | tf_op jit(solution)/shard_map/pallas_call | solution.py:243
  83.8 0.0 copy-start.4
  83.8 1.0 copy-done.4
  84.8 0.0 copy-start.8
  84.8 0.7 copy-done.8
  85.6 0.0 copy-start.1
  85.6 1.6 %reshape.25.w_ref = bf16[1024,192]{1,0:T(8,128)(2,1)S(1)} reshape(bf16[2,768,128]{2,1,0:T(8,128)(2,1)} %copy-done.8) | data formatting | bytes 786432 | tf_op jit(solution)/shard_map/reshape | solution.py:566
  87.2 0.0 copy-done.6
  87.2 0.0 copy-done.9
  87.2 0.0 copy-done.10
  87.2 0.0 copy-start.5
  87.2 1.2 copy-done.5
  88.4 25.4 %shard_map.87 = (bf16[4,512,128]{2,1,0:T(8,128)(2,1)S(1)}, bf16[16,64,1024]{2,1,0:T(8,128)(2,1)S(1)}) custom-call(bf16[8,64,1024]{2,1,0:T(8,128)(2,1)S(1)} %copy-done.5, bf16[1024,192]{1,0:T(8,128)(2,1)S(1)} %reshape.25.w_ref, bf16[8704,128]{1,0:T(8,128)(2,1)S(1)} %bitcast.4, bf16[64,4096]{1,0:T(8,128)(2,1)S(1)} %copy-done.6, bf16[64,512]{1,0:T(8,128)(2,1)S(1)} %copy-done.9, ...), custom_call_target="tpu_custom_call" | custom-call | tf_op jit(solution)/shard_map/pallas_call | solution.py:398
  113.9 0.0 copy-done.1
  113.9 0.0 copy-start.2
  113.9 1.3 copy-done.2
  115.2 0.0 copy-start.7
  115.2 0.8 copy-done.7
  116.0 13.8 %shard_map.88 = (bf16[64,4096]{1,0:T(8,128)(2,1)}, bf16[64,8192]{1,0:T(8,128)(2,1)}) custom-call(bf16[4,512,128]{2,1,0:T(8,128)(2,1)} %copy-done.7, bf16[1024,1024]{1,0:T(8,128)(2,1)} %bitcast.6, bf16[8704,128]{1,0:T(8,128)(2,1)} %bitcast.5), custom_call_target="tpu_custom_call" | custom-call | tf_op jit(solution)/shard_map/pallas_call | solution.py:517
  (2 shorter events, 0.0 us)
Async XLA Ops:
  1.6 4.1 %copy-start = (bf16[1,2686976]{1,0:T(2,128)(2,1)S(1)}, bf16[1,2686976]{1,0:T(2,128)(2,1)}, u32[]{:S(2)}) copy-start(bf16[1,2686976]{1,0:T(2,128)(2,1)} %pool_ref.1) | copy-start | bytes 16121860
  5.7 1.2 copy-start.3
  6.9 0.7 copy-start.11
  7.6 79.6 %copy-start.6 = (bf16[64,4096]{1,0:T(8,128)(2,1)S(1)}, bf16[64,4096]{1,0:T(8,128)(2,1)}, u32[]{:S(2)}) copy-start(bf16[64,4096]{1,0:T(8,128)(2,1)} %query_ref.1) | copy-start | bytes 1572868
  7.6 79.6 %copy-start.9 = (bf16[64,512]{1,0:T(8,128)(2,1)S(1)}, bf16[64,512]{1,0:T(8,128)(2,1)}, u32[]{:S(2)}) copy-start(bf16[64,512]{1,0:T(8,128)(2,1)} %key_ref.1) | copy-start | bytes 196612
  7.6 79.6 %copy-start.10 = (bf16[64,512]{1,0:T(8,128)(2,1)S(1)}, bf16[64,512]{1,0:T(8,128)(2,1)}, u32[]{:S(2)}) copy-start(bf16[64,512]{1,0:T(8,128)(2,1)} %value_ref.1) | copy-start | bytes 196612
  83.8 1.0 copy-start.4
  84.8 0.7 copy-start.8
  85.6 28.3 %copy-start.1 = (bf16[2,8,544,128]{3,2,1,0:T(8,128)(2,1)}, bf16[2,8,544,128]{3,2,1,0:T(8,128)(2,1)S(1)}, u32[]{:S(2)}) copy-start(bf16[2,8,544,128]{3,2,1,0:T(8,128)(2,1)S(1)} %get-tuple-element.9) | copy-start | bytes 6684676
  87.2 1.2 copy-start.5
  113.9 1.3 copy-start.2
  115.2 0.8 copy-start.7
